TPU v7x, 128 devices: a whole 4x4x4 slice. The times are simulated.
128 devices in a mesh: replica: 16 (over x_lo, z, core), shard: 8 (over y, x_hi).
Axes of the slice: x: 4 (x_hi: 2, x_lo: 2; x = x_hi * 2 + x_lo), y: 4, z: 4, core: 2. Of those that a mesh axis runs over, the one named last changes fastest.
Arguments:
- weights: bfloat16 [16, 2560, 7168], P('replica', None, 'shard'), may hold values from -60 to 60, as said below
- inputs: bfloat16 [8192, 2560], P('replica'), may hold values from -0.125 to 0.125
- targets: bfloat16 [8192, 7168], P('replica', 'shard'), may hold values from -6 to 6
- factors: float32 [3, 7168, 16], P(None, 'shard'), may hold values from -6 to 6
Outputs:
- mixed: bfloat16 [16, 2560, 7168], P('replica', None, 'shard')
Inputs may be any that keep to these rules, and one draw needn't show every extreme that they name: `weights`: independent entries for every replica.
All inputs are finite; a program needn't handle non-finite values.
Results may differ from a plain program's by a relative error of at most 0.0075.
Values may be sent and summed in bfloat16 or wider, within the bound.
A program may use at most 64 MiB of HBM per device.

v0:
```python
import jax
import jax.numpy as jnp
from jax import lax
from jax.sharding import PartitionSpec as P

ROUNDS = 3


DISTANCES = (1, 2, 4)
HIGH = lax.Precision.HIGHEST


def from_everyone(array, axis):
    devices = lax.axis_size(axis)
    return lax.all_to_all(
        jnp.broadcast_to(array[None], (devices, *array.shape)), axis, 0, 0, tiled=True
    )


def of_everyone(array, axis):
    return from_everyone(array, axis).sum(axis=0)


def passed_along(value, axis, steps):
    count = lax.axis_size(axis)
    pairs = [(source, (source + steps) % count) for source in range(count)]
    return lax.ppermute(value, axis, pairs)


def lower_solve(diff, gram):
    lower = jnp.linalg.cholesky(gram)
    solved = lax.linalg.triangular_solve(lower, diff, left_side=False, lower=True, transpose_a=True)
    return solved.astype(jnp.bfloat16)


def per_device(weights, inputs, targets, factors):
    weight = weights[0]
    for step in range(ROUNDS):
        dist = DISTANCES[step]
        output = jnp.dot(inputs, weight, preferred_element_type=jnp.float32)
        resid = (output - targets.astype(jnp.float32)).astype(jnp.bfloat16)
        grad = lax.dot_general(
            inputs, resid, (((0,), (0,)), ((), ())), preferred_element_type=jnp.float32
        )
        weight = (weight.astype(jnp.float32) - 0.3 * grad).astype(jnp.bfloat16)
        shared = factors[step].astype(jnp.bfloat16)
        left = of_everyone(jnp.dot(weight, shared, preferred_element_type=jnp.float32), "shard")
        diff = left - passed_along(left, "replica", dist)
        basis = lower_solve(diff, jnp.dot(diff.T, diff, precision=HIGH))
        right = lax.dot_general(
            weight, basis, (((0,), (0,)), ((), ())), preferred_element_type=jnp.float32
        )
        right_diff = right - passed_along(right, "replica", dist)
        delta = jnp.dot(
            basis, right_diff.astype(jnp.bfloat16).T, preferred_element_type=jnp.float32
        )
        weight = (weight.astype(jnp.float32) - 0.5 * delta).astype(jnp.bfloat16)
    return weight[None]


def solution(mesh):
    in_specs = (
        P("replica", None, "shard"),
        P("replica", None),
        P("replica", "shard"),
        P(None, "shard", None),
    )
    out_specs = P("replica", None, "shard")
    return jax.shard_map(
        per_device, mesh=mesh, in_specs=in_specs, out_specs=out_specs, check_vma=False
    )
```

profile of v0, /device:TPU:0, one launch (start us, length us, event | category | flops | bytes accessed | tf_op | source)
XLA Modules:
  0.0 208.8 jit_solution(18100376178031391623)
XLA Ops:
  0.0 0.0 copy-start
  0.0 1.1 convert.5
  1.1 7.3 %copy.16 = bf16[1,2560,896]{1,2,0:T(8,128)(2,1)} copy(bf16[1,2560,896]{2,1,0:T(8,128)(2,1)} %param.7) | data formatting | bytes 9175040 | tf_op args[0]
  8.4 0.0 copy-done
  8.4 11.5 %fusion.2 = bf16[2560,896]{0,1:T(8,128)(2,1)} fusion(bf16[512,2560]{1,0:T(8,128)(2,1)S(1)} %copy-done, bf16[1,2560,896]{1,2,0:T(8,128)(2,1)} %copy.16, bf16[512,896]{1,0:T(8,128)(2,1)} %param.9, bf16[1,2560,896]{2,1,0:T(8,128)(2,1)} %param.7), kind=kOutput, calls=%fused_computation.5 | convolution fusion | flops 4708171776 | bytes 17301504 | tf_op jit(solution)/shard_map/dot_general | solution.py:42
  19.9 3.0 %fusion.18 = f32[2560,16]{0,1:T(8,128)S(1)} fusion(bf16[2560,896]{0,1:T(8,128)(2,1)} %fusion.2, bf16[3,896,16]{1,2,0:T(8,128)(2,1)S(1)} %convert.5), kind=kOutput, calls=%fused_computation.32 | convolution fusion | flops 73400320 | bytes 4780032 | tf_op jit(solution)/shard_map/dot_general | solution.py:47
  22.9 0.1 broadcast_in_dim.9
  23.0 27.0 %all_to_all.15 = f32[8,2560,16]{1,2,0:T(8,128)} all-to-all(f32[8,2560,16]{1,2,0:T(8,128)S(1)} %broadcast_in_dim.9), channel_id=1, replica_groups=mesh['replica'=16,'shard'=8] {'shard'}, dimensions={0} | all-to-all | bytes 2621440 | tf_op jit(solution)/shard_map/all_to_all | solution.py:15
  50.0 1.4 reduce_sum.27
  51.4 0.1 collective-permute-start
  51.4 6.8 %collective-permute-done = f32[2560,16]{0,1:T(8,128)S(1)} collective-permute-done((f32[2560,16]{0,1:T(8,128)S(1)}, f32[2560,16]{0,1:T(8,128)S(1)}, u32[]{:S(2)}, u32[]{:S(2)}) %collective-permute-start) | collective-permute-done | bytes 163872 | tf_op jit(solution)/shard_map/ppermute | solution.py:27
  58.3 0.3 fusion.28
  58.6 0.1 copy.17
  58.7 1.5 cholesky.59
  60.2 0.7 compare_reduce_fusion.2
  60.9 0.7 fusion.19
  61.6 1.2 custom-call.7
  62.9 0.0 copy-start.2
  62.9 0.4 fusion.6
  63.2 3.8 %fusion.29 = f32[896,16]{0,1:T(8,128)S(1)} fusion(bf16[2560,896]{0,1:T(8,128)(2,1)} %fusion.2, bf16[2560,16]{0,1:T(8,128)(2,1)S(1)} %fusion.6), kind=kOutput, calls=%fused_computation.57 | convolution fusion | flops 73400320 | bytes 4726784 | tf_op jit(solution)/shard_map/dot_general | solution.py:50
  67.0 0.2 collective-permute-start.1
  67.2 5.7 %collective-permute-done.1 = f32[896,16]{0,1:T(8,128)S(1)} collective-permute-done((f32[896,16]{0,1:T(8,128)S(1)}, f32[896,16]{0,1:T(8,128)S(1)}, u32[]{:S(2)}, u32[]{:S(2)}) %collective-permute-start.1) | collective-permute-done | bytes 57376 | tf_op jit(solution)/shard_map/ppermute | solution.py:27
  72.9 0.0 copy-done.2
  72.9 3.5 %subtract_convert_fusion.2 = bf16[2560,896]{0,1:T(8,128)(2,1)} fusion(bf16[2560,896]{0,1:T(8,128)(2,1)S(1)} %copy-done.2, bf16[2560,16]{0,1:T(8,128)(2,1)S(1)} %fusion.6, f32[896,16]{0,1:T(8,128)S(1)} %fusion.29, f32[896,16]{0,1:T(8,128)S(1)} %collective-permute-done.1), kind=kOutput, calls=%fused_computation.8 | convolution fusion | flops 82604032 | bytes 9371648 | tf_op jit(solution)/shard_map/dot_general | solution.py:54
  76.4 11.4 %fusion.1 = bf16[2560,896]{0,1:T(8,128)(2,1)} fusion(bf16[2560,896]{0,1:T(8,128)(2,1)} %subtract_convert_fusion.2, bf16[512,2560]{1,0:T(8,128)(2,1)S(1)} %copy-done, bf16[512,896]{1,0:T(8,128)(2,1)} %param.9), kind=kOutput, calls=%fused_computation.3 | convolution fusion | flops 4708171776 | bytes 12713984 | tf_op jit(solution)/shard_map/dot_general | solution.py:42
  87.9 3.0 %fusion.17 = f32[2560,16]{0,1:T(8,128)S(1)} fusion(bf16[2560,896]{0,1:T(8,128)(2,1)} %fusion.1, bf16[3,896,16]{1,2,0:T(8,128)(2,1)S(1)} %convert.5), kind=kOutput, calls=%fused_computation.30 | convolution fusion | flops 73400320 | bytes 4780032 | tf_op jit(solution)/shard_map/dot_general | solution.py:47
  90.9 0.1 broadcast_in_dim.10
  91.0 19.1 %all_to_all.16 = f32[8,2560,16]{1,2,0:T(8,128)} all-to-all(f32[8,2560,16]{1,2,0:T(8,128)S(1)} %broadcast_in_dim.10), channel_id=1, replica_groups=mesh['replica'=16,'shard'=8] {'shard'}, dimensions={0} | all-to-all | bytes 2621440 | tf_op jit(solution)/shard_map/all_to_all | solution.py:15
  110.1 1.4 reduce_sum.28
  111.5 1.9 collective-permute-start.2
  113.4 5.7 %collective-permute-done.2 = f32[2560,16]{0,1:T(8,128)S(1)} collective-permute-done((f32[2560,16]{0,1:T(8,128)S(1)}, f32[2560,16]{0,1:T(8,128)S(1)}, u32[]{:S(2)}, u32[]{:S(2)}) %collective-permute-start.2) | collective-permute-done | bytes 163872 | tf_op jit(solution)/shard_map/ppermute | solution.py:27
  119.2 0.3 fusion.30
  119.5 0.1 copy.19
  119.5 1.5 cholesky.70
  121.1 0.6 compare_reduce_fusion.1
  121.7 0.6 fusion.20
  122.4 1.2 custom-call.8
  123.6 0.0 copy-start.3
  123.6 0.4 fusion.7
  124.0 3.8 %fusion.31 = f32[896,16]{0,1:T(8,128)S(1)} fusion(bf16[2560,896]{0,1:T(8,128)(2,1)} %fusion.1, bf16[2560,16]{0,1:T(8,128)(2,1)S(1)} %fusion.7), kind=kOutput, calls=%fused_computation.59 | convolution fusion | flops 73400320 | bytes 4726784 | tf_op jit(solution)/shard_map/dot_general | solution.py:50
  127.8 0.2 collective-permute-start.3
  128.0 6.3 %collective-permute-done.3 = f32[896,16]{0,1:T(8,128)S(1)} collective-permute-done((f32[896,16]{0,1:T(8,128)S(1)}, f32[896,16]{0,1:T(8,128)S(1)}, u32[]{:S(2)}, u32[]{:S(2)}) %collective-permute-start.3) | collective-permute-done | bytes 57376 | tf_op jit(solution)/shard_map/ppermute | solution.py:27
  134.2 0.0 copy-done.3
  134.3 3.5 %subtract_convert_fusion.1 = bf16[2560,896]{0,1:T(8,128)(2,1)} fusion(bf16[2560,896]{0,1:T(8,128)(2,1)S(1)} %copy-done.3, bf16[2560,16]{0,1:T(8,128)(2,1)S(1)} %fusion.7, f32[896,16]{0,1:T(8,128)S(1)} %fusion.31, f32[896,16]{0,1:T(8,128)S(1)} %collective-permute-done.3), kind=kOutput, calls=%fused_computation.7 | convolution fusion | flops 82604032 | bytes 9371648 | tf_op jit(solution)/shard_map/dot_general | solution.py:54
  137.8 11.4 %fusion = bf16[2560,896]{0,1:T(8,128)(2,1)} fusion(bf16[2560,896]{0,1:T(8,128)(2,1)} %subtract_convert_fusion.1, bf16[512,2560]{1,0:T(8,128)(2,1)S(1)} %copy-done, bf16[512,896]{1,0:T(8,128)(2,1)} %param.9), kind=kOutput, calls=%fused_computation.1 | convolution fusion | flops 4708171776 | bytes 12713984 | tf_op jit(solution)/shard_map/dot_general | solution.py:42
  149.2 3.0 %fusion.16 = f32[2560,16]{0,1:T(8,128)S(1)} fusion(bf16[2560,896]{0,1:T(8,128)(2,1)} %fusion, bf16[3,896,16]{1,2,0:T(8,128)(2,1)S(1)} %convert.5), kind=kOutput, calls=%fused_computation.28 | convolution fusion | flops 73400320 | bytes 4780032 | tf_op jit(solution)/shard_map/dot_general | solution.py:47
  152.2 0.1 broadcast_in_dim.11
  152.4 21.4 %all_to_all.17 = f32[8,2560,16]{1,2,0:T(8,128)} all-to-all(f32[8,2560,16]{1,2,0:T(8,128)S(1)} %broadcast_in_dim.11), channel_id=1, replica_groups=mesh['replica'=16,'shard'=8] {'shard'}, dimensions={0} | all-to-all | bytes 2621440 | tf_op jit(solution)/shard_map/all_to_all | solution.py:15
  173.8 1.4 reduce_sum.29
  175.2 0.1 collective-permute-start.4
  175.2 7.7 %collective-permute-done.4 = f32[2560,16]{0,1:T(8,128)S(1)} collective-permute-done((f32[2560,16]{0,1:T(8,128)S(1)}, f32[2560,16]{0,1:T(8,128)S(1)}, u32[]{:S(2)}, u32[]{:S(2)}) %collective-permute-start.4) | collective-permute-done | bytes 163872 | tf_op jit(solution)/shard_map/ppermute | solution.py:27
  183.0 0.3 fusion.32
  183.3 0.1 copy.21
  183.3 1.5 cholesky.81
  184.9 0.6 compare_reduce_fusion
  185.5 0.6 fusion.21
  186.2 1.2 custom-call.9
  187.4 0.4 fusion.8
  187.8 3.8 %fusion.33 = f32[896,16]{0,1:T(8,128)S(1)} fusion(bf16[2560,896]{0,1:T(8,128)(2,1)} %fusion, bf16[2560,16]{0,1:T(8,128)(2,1)S(1)} %fusion.8), kind=kOutput, calls=%fused_computation.61 | convolution fusion | flops 73400320 | bytes 4726784 | tf_op jit(solution)/shard_map/dot_general | solution.py:50
  191.5 0.0 collective-permute-start.5
  191.5 6.6 %collective-permute-done.5 = f32[896,16]{0,1:T(8,128)S(1)} collective-permute-done((f32[896,16]{0,1:T(8,128)S(1)}, f32[896,16]{0,1:T(8,128)S(1)}, u32[]{:S(2)}, u32[]{:S(2)}) %collective-permute-start.5) | collective-permute-done | bytes 57376 | tf_op jit(solution)/shard_map/ppermute | solution.py:27
  198.2 0.0 copy-done.1
  198.2 3.4 %fusion.3 = bf16[1,2560,896]{1,2,0:T(8,128)(2,1)} fusion(bf16[2560,16]{0,1:T(8,128)(2,1)S(1)} %fusion.8, bf16[2560,896]{0,1:T(8,128)(2,1)S(1)} %copy-done.1, f32[896,16]{0,1:T(8,128)S(1)} %fusion.33, f32[896,16]{0,1:T(8,128)S(1)} %collective-permute-done.5), kind=kOutput, calls=%fused_computation.9 | convolution fusion | flops 82604032 | bytes 9371648 | tf_op jit(solution)/shard_map/dot_general | solution.py:54
  201.6 7.2 %copy.23 = bf16[1,2560,896]{2,1,0:T(8,128)(2,1)} copy(bf16[1,2560,896]{1,2,0:T(8,128)(2,1)} %fusion.3) | data formatting | bytes 9175040 | tf_op jit(solution)/shard_map/broadcast_in_dim | solution.py:58
  (10 shorter events, 0.2 us)
Async XLA Ops:
  0.0 8.4 %copy-start = (bf16[512,2560]{1,0:T(8,128)(2,1)S(1)}, bf16[512,2560]{1,0:T(8,128)(2,1)}, u32[]{:S(2)}) copy-start(bf16[512,2560]{1,0:T(8,128)(2,1)} %param.8) | copy-start | bytes 7864324
  51.4 6.9 %collective-permute-start = (f32[2560,16]{0,1:T(8,128)S(1)}, f32[2560,16]{0,1:T(8,128)S(1)}, u32[]{:S(2)}, u32[]{:S(2)}) collective-permute-start(f32[2560,16]{0,1:T(8,128)S(1)} %reduce_sum.27), channel_id=1, source_target_pairs={{0,8},{8,16},{16,24},{24,32},{32,40},{40,48},{48,56},{56,64},{64,7... | collective-permute-start | bytes 491528 | tf_op jit(solution)/shard_map/ppermute | solution.py:27
  62.9 10.0 %copy-start.2 = (bf16[2560,896]{0,1:T(8,128)(2,1)S(1)}, bf16[2560,896]{0,1:T(8,128)(2,1)}, u32[]{:S(2)}) copy-start(bf16[2560,896]{0,1:T(8,128)(2,1)} %fusion.2) | copy-start | bytes 13762564
  67.0 5.9 %collective-permute-start.1 = (f32[896,16]{0,1:T(8,128)S(1)}, f32[896,16]{0,1:T(8,128)S(1)}, u32[]{:S(2)}, u32[]{:S(2)}) collective-permute-start(f32[896,16]{0,1:T(8,128)S(1)} %fusion.29), channel_id=1, source_target_pairs={{0,8},{8,16},{16,24},{24,32},{32,40},{40,48},{48,56},{56,64},{64,7... | collective-permute-start | bytes 172040 | tf_op jit(solution)/shard_map/ppermute | solution.py:27
  111.5 7.6 %collective-permute-start.2 = (f32[2560,16]{0,1:T(8,128)S(1)}, f32[2560,16]{0,1:T(8,128)S(1)}, u32[]{:S(2)}, u32[]{:S(2)}) collective-permute-start(f32[2560,16]{0,1:T(8,128)S(1)} %reduce_sum.28), channel_id=1, source_target_pairs={{0,16},{8,24},{16,32},{24,40},{32,48},{40,56},{48,64},{56,72},{64,... | collective-permute-start | bytes 491528 | tf_op jit(solution)/shard_map/ppermute | solution.py:27
  123.6 10.6 %copy-start.3 = (bf16[2560,896]{0,1:T(8,128)(2,1)S(1)}, bf16[2560,896]{0,1:T(8,128)(2,1)}, u32[]{:S(2)}) copy-start(bf16[2560,896]{0,1:T(8,128)(2,1)} %fusion.1) | copy-start | bytes 13762564
  127.8 6.5 %collective-permute-start.3 = (f32[896,16]{0,1:T(8,128)S(1)}, f32[896,16]{0,1:T(8,128)S(1)}, u32[]{:S(2)}, u32[]{:S(2)}) collective-permute-start(f32[896,16]{0,1:T(8,128)S(1)} %fusion.31), channel_id=1, source_target_pairs={{0,16},{8,24},{16,32},{24,40},{32,48},{40,56},{48,64},{56,72},{64,... | collective-permute-start | bytes 172040 | tf_op jit(solution)/shard_map/ppermute | solution.py:27
  175.2 7.8 %collective-permute-start.4 = (f32[2560,16]{0,1:T(8,128)S(1)}, f32[2560,16]{0,1:T(8,128)S(1)}, u32[]{:S(2)}, u32[]{:S(2)}) collective-permute-start(f32[2560,16]{0,1:T(8,128)S(1)} %reduce_sum.29), channel_id=1, source_target_pairs={{0,32},{8,40},{16,48},{24,56},{32,64},{40,72},{48,80},{56,88},{64,... | collective-permute-start | bytes 491528 | tf_op jit(solution)/shard_map/ppermute | solution.py:27
  187.4 10.8 %copy-start.1 = (bf16[2560,896]{0,1:T(8,128)(2,1)S(1)}, bf16[2560,896]{0,1:T(8,128)(2,1)}, u32[]{:S(2)}) copy-start(bf16[2560,896]{0,1:T(8,128)(2,1)} %fusion) | copy-start | bytes 13762564
  191.5 6.6 %collective-permute-start.5 = (f32[896,16]{0,1:T(8,128)S(1)}, f32[896,16]{0,1:T(8,128)S(1)}, u32[]{:S(2)}, u32[]{:S(2)}) collective-permute-start(f32[896,16]{0,1:T(8,128)S(1)} %fusion.33), channel_id=1, source_target_pairs={{0,32},{8,40},{16,48},{24,56},{32,64},{40,72},{48,80},{56,88},{64,... | collective-permute-start | bytes 172040 | tf_op jit(solution)/shard_map/ppermute | solution.py:27
where the time goes:
time: 210 us; the launch traced here: 209 us
  blocking collectives  67.5 us (32%)
  matrix products  67.1 us (32%)
  waiting for transfers between devices  38.9 us (19%)
  other arithmetic  17.7 us (8%)
  local copies, waits for them, and re-layouts  15.1 us (7%)
  starting transfers between devices  2.44 us (1%)
    all_to_all x3, blocking collectives, from_everyone(): lax.all_to_all(jnp.broadcast_to(array[None], (devices, *array.shape)), ax...  67.5 us
    ppermute x6, waiting for transfers between devices, passed_along(): return lax.ppermute(value, axis, pairs)  38.9 us
    dot_general x3, matrix products, per_device(): lax.dot_general(inputs, resid, (((0,), (0,)), ((), ())), preferred_elemen...  34.4 us
    dot_general x3, matrix products, per_device(): lax.dot_general(weight, basis, (((0,), (0,)), ((), ())), preferred_elemen...  11.3 us
    dot_general x3, matrix products, per_device(): jnp.dot(basis, right_diff.astype(jnp.bfloat16).T, preferred_element_type=...  10.5 us
    dot_general x3, matrix products, per_device(): jnp.dot(weight, shared, preferred_element_type=jnp.float32)  9.01 us
    unnamed x9, local copies, waits for them, and re-layouts  7.31 us
    broadcast_in_dim x1, local copies, waits for them, and re-layouts, per_device(): return weight[None]  7.17 us
  transfers between devices with their start and end apart: 6, of which 6 were waited for; matrix products, arithmetic and copies ran while one was open for 0% of the time, Pallas kernels for 0%

commit v1 on v0

v1 whole, which is shorter than its diff:
```python
import jax
import jax.numpy as jnp
from jax import lax
from jax.sharding import PartitionSpec as P

ROUNDS = 3
RANK = 16
DISTANCES = (1, 2, 4)
HIGH = lax.Precision.HIGHEST
F32, BF16 = jnp.float32, jnp.bfloat16
NT = (((1,), (1,)), ((), ()))
NN = (((1,), (0,)), ((), ()))
TN = (((0,), (0,)), ((), ()))


def mm(a, b, dims):
    return lax.dot_general(a.astype(BF16), b.astype(BF16), dims, preferred_element_type=F32)


def passed_along(value, axis, steps):
    count = lax.axis_size(axis)
    pairs = [(source, (source + steps) % count) for source in range(count)]
    return lax.ppermute(value, axis, pairs)


def orthonormal(diff):
    gram = lax.dot_general(diff, diff, NT, precision=HIGH, preferred_element_type=F32)
    lower = jnp.linalg.cholesky(gram)
    solved = lax.linalg.triangular_solve(lower, diff, left_side=True, lower=True)
    return solved.astype(BF16)


def per_device(weights, x, targets, factors):
    weight = weights[0]
    qb = factors.astype(BF16).transpose(0, 2, 1).reshape(ROUNDS * RANK, -1)
    partial = jnp.concatenate([mm(qb, weight, NT), mm(qb, targets, NT)], axis=1)
    total = lax.psum(partial, "shard")
    depth = weight.shape[0]
    shared, goal = total[:, :depth], total[:, depth:]

    first = mm(x, weight, NN) - targets.astype(F32)
    gram_x = mm(x, x, NT)
    sums = [first]
    for _ in range(ROUNDS - 1):
        sums.append(first + sums[-1] - 0.3 * mm(gram_x, sums[-1], NN))
    grown = weight.astype(F32) - 0.3 * mm(x, sums[-1], TN)

    bases, rights = [], []
    for step in range(ROUNDS):
        dist = DISTANCES[step]
        shared = shared - 0.3 * mm(mm(shared, x, NT) - goal, x, NN)
        left = shared[:RANK]
        basis = orthonormal(left - passed_along(left, "replica", dist))
        shared, goal = shared[RANK:], goal[RANK:]
        if step < ROUNDS - 1:
            inner = mm(shared, basis, NT)
            inner = inner - passed_along(inner, "replica", dist)
            shared = shared - 0.5 * mm(inner, basis, NN)
        inside = mm(basis, x, NT)
        right = mm(basis, weight, NN) - 0.3 * mm(inside, sums[step], NN)
        for old, old_right in zip(bases, rights):
            right = right - 0.5 * mm(mm(basis, old, NT), old_right, NN)
        rights.append(right - passed_along(right, "replica", dist))
        bases.append(basis)
        if step < ROUNDS - 1:
            bases = [old.astype(F32) - 0.3 * mm(mm(old, x, NT), x, NN) for old in bases]
    low_rank = mm(jnp.concatenate([b.astype(F32) for b in bases]), jnp.concatenate(rights), TN)
    return (grown - 0.5 * low_rank).astype(BF16)[None]


def solution(mesh):
    in_specs = (
        P("replica", None, "shard"),
        P("replica", None),
        P("replica", "shard"),
        P(None, "shard", None),
    )
    out_specs = P("replica", None, "shard")
    return jax.shard_map(
        per_device, mesh=mesh, in_specs=in_specs, out_specs=out_specs, check_vma=False
    )
```

time: 210 us -> 218 us (1.038)
  blocking collectives: 67.5 us -> 0 us
  waiting for transfers between devices: 38.9 us -> 103 us
  between operations: 0.15 us -> 13.7 us
  matrix products: 67.1 us -> 64.7 us
    psum x0 -> x1, waiting for transfers between devices: none -> 80.1 us  [per_device(): total = lax.psum(partial, 'shard')]
    all_to_all x3 -> x0, blocking collectives: 67.5 us -> none  [from_everyone(): lax.all_to_all(jnp.broadcast_to(array[None], (devices, *array.shape)), ax...]
    ppermute x6 -> x8, waiting for transfers between devices: 38.9 us -> 23.2 us  [passed_along(): return lax.ppermute(value, axis, pairs)]
    reduce_sum x3 -> x0, other arithmetic: 4.19 us -> none  [of_everyone(): return from_everyone(array, axis).sum(axis=0)]
    dot_general x15 -> x32, matrix products: 66 us -> 62.7 us  [the longest x29 61.9 us: mm(): lax.dot_general(a.astype(BF16), b.astype(BF16), dims, preferred_element_t...]
    unnamed x9 -> x33, local copies, waits for them, and re-layouts: 7.31 us -> 9.72 us
    another operation x16 -> x18, other arithmetic: 13.4 us -> 15.3 us  [the longest x9 7.34 us: orthonormal(): lower = jnp.linalg.cholesky(gram)]
    broadcast_in_dim x4 -> x1, local copies, waits for them, and re-layouts: 7.55 us -> 7.17 us  [per_device(): return (grown - 0.5 * low_rank).astype(BF16)[None]]
  transfers between devices with their start and end apart: 6 -> 9, of which waited for: 6 -> 6; matrix products, arithmetic and copies ran while one was open for 0% -> 17% of each run, Pallas kernels for 0% -> 0%
where the time goes in v1:
time: 218 us; the launch traced here: 217 us
  waiting for transfers between devices  103 us (47%)
  matrix products  64.7 us (30%)
  other arithmetic  17.9 us (8%)
  local copies, waits for them, and re-layouts  17.1 us (8%)
  between operations  13.7 us (6%)
    psum x1, waiting for transfers between devices, per_device(): total = lax.psum(partial, 'shard')  80.1 us
    dot_general x29, matrix products, mm(): lax.dot_general(a.astype(BF16), b.astype(BF16), dims, preferred_element_t...  61.9 us
    ppermute x8, waiting for transfers between devices, passed_along(): return lax.ppermute(value, axis, pairs)  23.2 us
    unnamed x33, local copies, waits for them, and re-layouts  9.72 us
    another operation x9, other arithmetic, orthonormal(): lower = jnp.linalg.cholesky(gram)  7.34 us
    broadcast_in_dim x1, local copies, waits for them, and re-layouts, per_device(): return (grown - 0.5 * low_rank).astype(BF16)[None]  7.17 us
    another operation x6, other arithmetic, orthonormal(): lax.linalg.triangular_solve(lower, diff, left_side=True, lower=True)  5.65 us
  transfers between devices with their start and end apart: 9, of which 6 were waited for; matrix products, arithmetic and copies ran while one was open for 17% of the time, Pallas kernels for 0%

profile of v1, /device:TPU:0, one launch (start us, length us, event | category | flops | bytes accessed | tf_op | source)
XLA Modules:
  0.0 217.2 jit_solution(6847564169925928657)
XLA Ops:
  6.5 1.1 convert_element_type.114
  7.6 3.9 %fusion.9 = f32[48,2560]{1,0:T(8,128)S(1)} fusion(bf16[48,896]{1,0:T(8,128)(2,1)S(1)} %bitcast.108, bf16[1,2560,896]{2,1,0:T(8,128)(2,1)} %param.7), kind=kOutput, calls=%fused_computation.10 | convolution fusion | flops 220200960 | bytes 5165056 | tf_op jit(solution)/shard_map/dot_general | solution.py:17
  11.5 0.4 fusion.72
  11.9 0.9 pad_maximum_fusion
  12.8 5.2 %convert_subtract_fusion = f32[512,896]{1,0:T(8,128)S(1)} fusion(bf16[512,896]{1,0:T(8,128)(2,1)S(1)} %copy-done.8, bf16[512,2560]{1,0:T(8,128)(2,1)S(1)} %copy-done, bf16[1,2560,896]{2,1,0:T(8,128)(2,1)} %param.7), kind=kOutput, calls=%fused_computation.34 | convolution fusion | flops 2349727744 | bytes 9961472 | tf_op jit(solution)/shard_map/dot_general | solution.py:17
  18.0 1.5 convolution_convert_fusion.3
  19.6 0.8 copy-done.11
  20.4 2.0 multiply_subtract_fusion
  22.3 80.1 %all-reduce.2.cloned.1.call-done = f32[48,3072]{1,0:T(8,128)} async-done(((f32[48,3072]{1,0:T(8,128)}), f32[48,3072]{1,0:T(8,128)}) %all-reduce.2.cloned.1.call-update) | async-done | bytes 589840 | tf_op jit(solution)/shard_map/psum | solution.py:37
  102.4 2.6 %fusion.13 = f32[48,2560]{1,0:T(8,128)S(1)} fusion(bf16[512,2560]{1,0:T(8,128)(2,1)S(1)} %copy-done, f32[48,3072]{1,0:T(8,128)} %all-reduce.2.cloned.1.call-done), kind=kOutput, calls=%fused_computation.15 | convolution fusion | flops 252076032 | bytes 6815744 | tf_op jit(solution)/shard_map/dot_general | solution.py:17
  105.2 4.4 %subtract_convert_fusion = bf16[512,896]{1,0:T(8,128)(2,1)} fusion(f32[512,896]{1,0:T(8,128)} %copy-done.2, f32[512,896]{1,0:T(8,128)} %multiply_subtract_fusion, bf16[512,512]{1,0:T(8,128)(2,1)} %copy-done.11), kind=kOutput, calls=%fused_computation.32 | convolution fusion | flops 472055808 | bytes 5111808 | tf_op jit(solution)/shard_map/dot_general | solution.py:17
  109.6 2.4 %collective-permute-done = f32[16,2560]{1,0:T(8,128)S(1)} collective-permute-done((f32[16,2560]{1,0:T(8,128)S(1)}, f32[16,2560]{1,0:T(8,128)S(1)}, u32[]{:S(2)}, u32[]{:S(2)}) %collective-permute-start) | collective-permute-done | bytes 163872 | tf_op jit(solution)/shard_map/ppermute | solution.py:23
  112.0 0.3 fusion.70
  112.4 1.5 cholesky.59
  113.9 0.7 compare_reduce_fusion.2
  114.6 0.6 fusion.59
  115.3 1.2 custom-call.7
  116.5 0.4 convolution_convert_fusion.2
  117.0 3.0 %fusion.7 = f32[16,896]{1,0:T(8,128)S(1)} fusion(bf16[16,2560]{1,0:T(8,128)(2,1)S(1)} %convolution_convert_fusion.2, bf16[1,2560,896]{2,1,0:T(8,128)(2,1)} %param.7), kind=kOutput, calls=%fused_computation.8 | convolution fusion | flops 73400320 | bytes 4726784 | tf_op jit(solution)/shard_map/dot_general | solution.py:17
  120.1 0.8 convolution_convert_fusion.7
  120.8 0.5 convolution_multiply_fusion.6
  121.3 0.2 copy-done.3
  121.6 0.9 fusion.28
  122.5 1.8 fusion.19
  124.3 1.7 collective-permute-done.1
  126.0 1.0 fusion.15
  127.0 2.5 %fusion.14 = f32[32,2560]{1,0:T(8,128)S(1)} fusion(f32[32,2560]{1,0:T(8,128)} %fusion.15, bf16[512,2560]{1,0:T(8,128)(2,1)S(1)} %copy-done, f32[48,3072]{1,0:T(8,128)} %all-reduce.2.cloned.1.call-done), kind=kOutput, calls=%fused_computation.17 | convolution fusion | flops 168050688 | bytes 6291456 | tf_op jit(solution)/shard_map/dot_general | solution.py:17
  129.6 0.9 subtract_convert_fusion.4
  130.5 6.5 %collective-permute-done.2 = f32[16,2560]{1,0:T(8,128)S(1)} collective-permute-done((f32[16,2560]{1,0:T(8,128)S(1)}, f32[16,2560]{1,0:T(8,128)S(1)}, u32[]{:S(2)}, u32[]{:S(2)}) %collective-permute-start.2) | collective-permute-done | bytes 163872 | tf_op jit(solution)/shard_map/ppermute | solution.py:23
  137.0 0.3 fusion.69
  137.4 1.5 cholesky.70
  139.0 0.6 compare_reduce_fusion.1
  139.6 0.6 fusion.60
  140.3 1.2 custom-call.8
  141.5 0.4 convolution_convert_fusion.1
  141.8 3.0 %fusion.5 = f32[16,896]{1,0:T(8,128)S(1)} fusion(bf16[16,2560]{1,0:T(8,128)(2,1)S(1)} %convolution_convert_fusion.1, bf16[1,2560,896]{2,1,0:T(8,128)(2,1)} %param.7), kind=kOutput, calls=%fused_computation.6 | convolution fusion | flops 73400320 | bytes 4726784 | tf_op jit(solution)/shard_map/dot_general | solution.py:17
  144.9 0.8 convolution_convert_fusion.5
  145.6 0.1 fusion.54
  145.8 1.1 subtract_convert_fusion.1
  146.9 0.2 fusion.27
  147.1 0.2 collective-permute-start.3
  147.4 0.3 fusion.26
  147.8 5.4 %collective-permute-done.3 = f32[16,16]{1,0:T(8,128)S(1)} collective-permute-done((f32[16,16]{1,0:T(8,128)S(1)}, f32[16,16]{1,0:T(8,128)S(1)}, u32[]{:S(2)}, u32[]{:S(2)}) %collective-permute-start.3) | collective-permute-done | bytes 1056 | tf_op jit(solution)/shard_map/ppermute | solution.py:23
  153.3 2.0 fusion.16
  155.3 0.6 subtract_convert_fusion.3
  155.9 7.1 %collective-permute-done.4 = f32[16,2560]{1,0:T(8,128)S(1)} collective-permute-done((f32[16,2560]{1,0:T(8,128)S(1)}, f32[16,2560]{1,0:T(8,128)S(1)}, u32[]{:S(2)}, u32[]{:S(2)}) %collective-permute-start.4) | collective-permute-done | bytes 163872 | tf_op jit(solution)/shard_map/ppermute | solution.py:23
  163.0 0.7 copy-done.7
  163.7 0.3 fusion.73
  164.0 0.7 fusion.63
  164.7 2.1 cholesky.81
  166.9 0.7 compare_reduce_fusion
  167.6 0.7 fusion.61
  168.3 1.2 custom-call.9
  169.5 1.3 convolution_convert_fusion
  170.8 0.6 copy-done.5
  171.4 3.6 %fusion.3 = f32[16,896]{1,0:T(8,128)} fusion(bf16[16,2560]{1,0:T(8,128)(2,1)S(1)} %convolution_convert_fusion, bf16[1,2560,896]{2,1,0:T(8,128)(2,1)} %param.7), kind=kOutput, calls=%fused_computation.4 | convolution fusion | flops 73400320 | bytes 4726784 | tf_op jit(solution)/shard_map/dot_general | solution.py:17
  175.0 2.5 %fusion.25 = f32[16,896]{1,0:T(8,128)} fusion(f32[16,896]{1,0:T(8,128)} %fusion.3, bf16[512,896]{1,0:T(8,128)(2,1)S(1)} %copy-done.4, bf16[16,2560]{1,0:T(8,128)(2,1)} %copy-done.5, bf16[512,2560]{1,0:T(8,128)(2,1)S(1)} %copy-done), kind=kOutput, calls=%fused_computation.44 | convolution fusion | flops 56659968 | bytes 3735552 | tf_op jit(solution)/shard_map/dot_general | solution.py:17
  177.6 1.8 fusion.24
  179.4 1.8 fusion.23
  181.3 6.1 %fusion.71 = f32[896,2560]{1,0:T(8,128)} fusion(bf16[512,896]{1,0:T(8,128)(2,1)S(1)} %copy-done.4, bf16[512,2560]{1,0:T(8,128)(2,1)S(1)} %copy-done), kind=kOutput, calls=%fused_computation.122 | convolution fusion | flops 2348810240 | bytes 12713984 | tf_op jit(solution)/shard_map/dot_general | solution.py:17
  187.4 7.3 %copy.5 = bf16[1,2560,896]{1,2,0:T(8,128)(2,1)} copy(bf16[1,2560,896]{2,1,0:T(8,128)(2,1)} %param.7) | data formatting | bytes 9175040 | tf_op args[0]
  194.8 0.8 subtract_convert_fusion.2
  195.6 7.5 %fusion.2 = bf16[1,2560,896]{1,2,0:T(8,128)(2,1)} fusion(f32[896,2560]{1,0:T(8,128)} %fusion.71, bf16[1,2560,896]{1,2,0:T(8,128)(2,1)} %copy.5, bf16[16,2560]{1,0:T(8,128)(2,1)S(1)} %copy-done.6, bf16[16,2560]{1,0:T(8,128)(2,1)S(1)} %copy-done.9, bf16[16,2560]{1,0:T(8,128)(2,1)S(1)} %copy-done.10, bf16[16,896]{1,0:T(8,128)(2,1)S(1)} %subtract_convert_fusion.2, ...), kind=kOutput, calls=%fused_computation.3 | convolution fusion | flops 234958848 | bytes 18681856 | tf_op jit(solution)/shard_map/dot_general | solution.py:17
  203.2 7.2 %copy.10 = bf16[1,2560,896]{2,1,0:T(8,128)(2,1)} copy(bf16[1,2560,896]{1,2,0:T(8,128)(2,1)} %fusion.2) | data formatting | bytes 9175040 | tf_op jit(solution)/shard_map/broadcast_in_dim | solution.py:68
  (53 shorter events, 1.0 us)
Async XLA Ops:
  6.5 6.3 %copy-start = (bf16[512,2560]{1,0:T(8,128)(2,1)S(1)}, bf16[512,2560]{1,0:T(8,128)(2,1)}, u32[]{:S(2)}) copy-start(bf16[512,2560]{1,0:T(8,128)(2,1)} %param.8) | copy-start | bytes 7864324
  6.5 95.9 %all-reduce.2.cloned.1.call-start = ((), (), s32[]{:S(2)}) async-start(), calls=%async_computation | async-start | bytes 1179648 | tf_op jit(solution)/shard_map/psum | solution.py:37
  7.6 3.9 %copy-start.8 = (bf16[512,896]{1,0:T(8,128)(2,1)S(1)}, bf16[512,896]{1,0:T(8,128)(2,1)}, u32[]{:S(2)}) copy-start(bf16[512,896]{1,0:T(8,128)(2,1)} %param.9) | copy-start | bytes 2752516
  18.0 1.6 copy-start.2
  19.6 0.8 copy-start.11
  105.1 6.9 %collective-permute-start = (f32[16,2560]{1,0:T(8,128)S(1)}, f32[16,2560]{1,0:T(8,128)S(1)}, u32[]{:S(2)}, u32[]{:S(2)}) collective-permute-start(f32[16,2560]{1,0:T(8,128)S(1)} %slice.42), channel_id=1, source_target_pairs={{0,8},{8,16},{16,24},{24,32},{32,40},{40,48},{48,56},{56,64},{64,7... | collective-permute-start | bytes 491528 | tf_op jit(solution)/shard_map/ppermute | solution.py:23
  120.0 1.5 copy-start.3
  120.8 5.2 %collective-permute-start.1 = (f32[32,16]{0,1:T(8,128)S(1)}, f32[32,16]{0,1:T(8,128)S(1)}, u32[]{:S(2)}, u32[]{:S(2)}) collective-permute-start(f32[32,16]{0,1:T(8,128)S(1)} %fusion.40), channel_id=1, source_target_pairs={{0,8},{8,16},{16,24},{24,32},{32,40},{40,48},{48,56},{56,64},{64,7... | collective-permute-start | bytes 6152 | tf_op jit(solution)/shard_map/ppermute | solution.py:23
  122.4 7.2 %collective-permute-start.5 = (f32[16,896]{1,0:T(8,128)}, f32[16,896]{1,0:T(8,128)}, u32[]{:S(2)}, u32[]{:S(2)}) collective-permute-start(f32[16,896]{1,0:T(8,128)} %fusion.28), channel_id=1, source_target_pairs={{0,8},{8,16},{16,24},{24,32},{32,40},{40,48},{48,56},{56,64},{64,7... | collective-permute-start | bytes 172040 | tf_op jit(solution)/shard_map/ppermute | solution.py:23
  129.5 7.5 %collective-permute-start.2 = (f32[16,2560]{1,0:T(8,128)S(1)}, f32[16,2560]{1,0:T(8,128)S(1)}, u32[]{:S(2)}, u32[]{:S(2)}) collective-permute-start(f32[16,2560]{1,0:T(8,128)S(1)} %slice.45), channel_id=1, source_target_pairs={{0,16},{8,24},{16,32},{24,40},{32,48},{40,56},{48,64},{56,72},{64,... | collective-permute-start | bytes 491528 | tf_op jit(solution)/shard_map/ppermute | solution.py:23
  130.5 16.9 %copy-start.12 = (bf16[16,896]{1,0:T(8,128)(2,1)}, bf16[16,896]{1,0:T(8,128)(2,1)S(1)}, u32[]{:S(2)}) copy-start(bf16[16,896]{1,0:T(8,128)(2,1)S(1)} %subtract_convert_fusion.4) | copy-start | bytes 86020
  144.9 2.1 copy-start.1
  147.1 6.0 %collective-permute-start.3 = (f32[16,16]{1,0:T(8,128)S(1)}, f32[16,16]{1,0:T(8,128)S(1)}, u32[]{:S(2)}, u32[]{:S(2)}) collective-permute-start(f32[16,16]{1,0:T(8,128)S(1)} %fusion.54), channel_id=1, source_target_pairs={{0,16},{8,24},{16,32},{24,40},{32,48},{40,56},{48,64},{56,72},{64,... | collective-permute-start | bytes 3080 | tf_op jit(solution)/shard_map/ppermute | solution.py:23
  147.7 7.6 %collective-permute-start.6 = (f32[16,896]{1,0:T(8,128)S(1)}, f32[16,896]{1,0:T(8,128)S(1)}, u32[]{:S(2)}, u32[]{:S(2)}) collective-permute-start(f32[16,896]{1,0:T(8,128)S(1)} %fusion.26), channel_id=1, source_target_pairs={{0,16},{8,24},{16,32},{24,40},{32,48},{40,56},{48,64},{56,72},{64,... | collective-permute-start | bytes 172040 | tf_op jit(solution)/shard_map/ppermute | solution.py:23
  155.3 7.7 %collective-permute-start.4 = (f32[16,2560]{1,0:T(8,128)S(1)}, f32[16,2560]{1,0:T(8,128)S(1)}, u32[]{:S(2)}, u32[]{:S(2)}) collective-permute-start(f32[16,2560]{1,0:T(8,128)S(1)} %fusion.16), channel_id=1, source_target_pairs={{0,32},{8,40},{16,48},{24,56},{32,64},{40,72},{48,80},{56,88},{64,... | collective-permute-start | bytes 491528 | tf_op jit(solution)/shard_map/ppermute | solution.py:23
  163.0 0.7 copy-start.7
  163.7 11.4 %copy-start.4 = (bf16[512,896]{1,0:T(8,128)(2,1)S(1)}, bf16[512,896]{1,0:T(8,128)(2,1)}, u32[]{:S(2)}) copy-start(bf16[512,896]{1,0:T(8,128)(2,1)} %subtract_convert_fusion) | copy-start | bytes 2752516
  170.8 0.6 copy-start.5
  181.3 13.5 %collective-permute-start.7 = (f32[16,896]{1,0:T(8,128)}, f32[16,896]{1,0:T(8,128)}, u32[]{:S(2)}, u32[]{:S(2)}) collective-permute-start(f32[16,896]{1,0:T(8,128)} %fusion.23), channel_id=1, source_target_pairs={{0,32},{8,40},{16,48},{24,56},{32,64},{40,72},{48,80},{56,88},{64,... | collective-permute-start | bytes 172040 | tf_op jit(solution)/shard_map/ppermute | solution.py:23
  187.4 7.4 %copy-start.15 = (f32[16,896]{1,0:T(8,128)S(1)}, f32[16,896]{1,0:T(8,128)}, u32[]{:S(2)}) copy-start(f32[16,896]{1,0:T(8,128)} %fusion.23) | copy-start | bytes 172036
  187.4 8.2 %copy-start.6 = (bf16[16,2560]{1,0:T(8,128)(2,1)S(1)}, bf16[16,2560]{1,0:T(8,128)(2,1)}, u32[]{:S(2)}) copy-start(bf16[16,2560]{1,0:T(8,128)(2,1)} %copy-done.5) | copy-start | bytes 245764
  187.4 8.2 %copy-start.9 = (bf16[16,2560]{1,0:T(8,128)(2,1)S(1)}, bf16[16,2560]{1,0:T(8,128)(2,1)}, u32[]{:S(2)}) copy-start(bf16[16,2560]{1,0:T(8,128)(2,1)} %subtract_convert_fusion.1) | copy-start | bytes 245764
  187.4 8.2 %copy-start.10 = (bf16[16,2560]{1,0:T(8,128)(2,1)S(1)}, bf16[16,2560]{1,0:T(8,128)(2,1)}, u32[]{:S(2)}) copy-start(bf16[16,2560]{1,0:T(8,128)(2,1)} %fusion.19) | copy-start | bytes 245764
  187.4 8.2 %copy-start.13 = (bf16[16,896]{1,0:T(8,128)(2,1)S(1)}, bf16[16,896]{1,0:T(8,128)(2,1)}, u32[]{:S(2)}) copy-start(bf16[16,896]{1,0:T(8,128)(2,1)} %copy-done.12) | copy-start | bytes 86020
  187.4 8.2 %copy-start.14 = (bf16[16,896]{1,0:T(8,128)(2,1)S(1)}, bf16[16,896]{1,0:T(8,128)(2,1)}, u32[]{:S(2)}) copy-start(bf16[16,896]{1,0:T(8,128)(2,1)} %subtract_convert_fusion.3) | copy-start | bytes 86020
Sparse Core Ops, SparseCore 0:
  12.9 89.4 all-reduce.1

commit v2 on v1

v2 whole, which is shorter than its diff:
```python
import jax
import jax.numpy as jnp
from jax import lax
from jax.experimental import pallas as pl
from jax.experimental.pallas import tpu as pltpu
from jax.sharding import PartitionSpec as P

RANK = 16
DISTANCES = (1, 2, 4)
HIGH = lax.Precision.HIGHEST
F32, BF16 = jnp.float32, jnp.bfloat16
NT = (((1,), (1,)), ((), ()))
NN = (((1,), (0,)), ((), ()))
TN = (((0,), (0,)), ((), ()))
MESH = pl.DeviceIdType.MESH
CHUNK = 512


def mm(a, b, dims):
    return lax.dot_general(a.astype(BF16), b.astype(BF16), dims, preferred_element_type=F32)


def stacked(value):
    high = value.astype(BF16)
    rest = (value - high.astype(F32)).astype(BF16)
    return jnp.concatenate([high, rest], axis=0)


def folded(product):
    half = product.shape[0] // 2
    return product[:half] + product[half:]


def fine(value, matrix, dims):
    return folded(lax.dot_general(stacked(value), matrix, dims, preferred_element_type=F32))


def inverse_factor(gram):
    lane = lax.broadcasted_iota(jnp.int32, (RANK, RANK), 1)
    row = lax.broadcasted_iota(jnp.int32, (RANK, RANK), 0)
    below = lax.broadcasted_iota(jnp.int32, (RANK, 1), 0)
    inverse = jnp.where(lane == row, 1.0, 0.0).astype(F32)
    pivots = jnp.ones((RANK, 1), F32)
    for j in range(RANK):
        pivot = gram[j : j + 1, j : j + 1]
        factor = jnp.where(below > j, gram[:, j : j + 1] / pivot, 0.0)
        pivots = jnp.where(below == j, pivot, pivots)
        inverse = inverse - factor * inverse[j : j + 1, :]
        gram = gram - factor * gram[j : j + 1, :]
    return lax.rsqrt(pivots) * inverse


def orthonormal(diff):
    gram = lax.dot_general(diff, diff, NT, precision=HIGH, preferred_element_type=F32)
    inverse = inverse_factor(gram)
    basis = lax.dot_general(inverse, diff, NN, precision=HIGH, preferred_element_type=F32)
    return basis.astype(BF16)


def make_kernel(replicas, shards, depth, hidden, tokens):
    wide = depth + tokens
    lanes = wide // shards
    part_lanes = depth // (shards // 2)

    def kernel(
        w_hbm, x_hbm, t_hbm, f_ref, grown_hbm, bases_ref, rights_ref,
        w, x, t, first, sums, gram_x, grown,
        part0, part1, rs0, rs1, own0, own1, p_own, p_in, v12, c_out, c_in, q_out, q_in,
        load_sem, rs_send, rs_recv, ag_send, ag_recv, x_send, x_recv,
    ):
        r, s = lax.axis_index("replica"), lax.axis_index("shard")

        def peer(dr, ds):
            return (lax.rem(r + (dr + replicas), replicas), lax.rem(s + ds, shards))

        def load(source, target, number):
            return pltpu.make_async_copy(source, target, load_sem.at[number])

        def send(source, target, send_sem, recv_sem, where):
            return pltpu.make_async_remote_copy(
                src_ref=source, dst_ref=target, send_sem=send_sem, recv_sem=recv_sem,
                device_id=where, device_id_type=MESH,
            )

        chunks = depth // CHUNK
        loads = [
            load(w_hbm.at[pl.ds(c * CHUNK, CHUNK)], w.at[pl.ds(c * CHUNK, CHUNK)], c)
            for c in range(chunks)
        ] + [load(t_hbm, t, chunks), load(x_hbm, x, chunks + 1)]
        for copy in loads:
            copy.start()

        barrier = pltpu.get_barrier_semaphore()
        friends = [(0, o) for o in range(1, shards)]
        friends += [(1, o) for o in range(shards)] + [(-1, o) for o in range(shards)]
        friends += [(2, 0), (-2, 0), (4, 0), (-4, 0)]
        for dr, ds in friends:
            pl.semaphore_signal(barrier, inc=1, device_id=peer(dr, ds), device_id_type=MESH)

        c_out[...] = jnp.zeros_like(c_out)
        shared = f_ref[...].astype(BF16)
        images = []
        for c in range(chunks):
            loads[c].wait()
            images.append(lax.dot_general(shared, w[c * CHUNK : (c + 1) * CHUNK, :], NT, preferred_element_type=F32))
        loads[chunks].wait()
        goal = lax.dot_general(shared, t[...], NT, preferred_element_type=F32)
        loads[chunks + 1].wait()
        image = jnp.concatenate(images, axis=1)

        def stepped(value, aim):
            off = fine(value, x[...], NT) - aim
            return value - 0.3 * fine(off, x[...], NN)

        image = stepped(image, goal)
        part0[...] = image[:RANK]
        part1[:, :depth] = image[RANK:]
        part1[:, depth:] = goal[RANK:]

        def piece0(ref, index):
            rows = pl.multiple_of(lax.rem(index, 2) * 8, 8)
            columns = pl.multiple_of((index // 2) * part_lanes, 128)
            return ref.at[pl.ds(rows, 8), pl.ds(columns, part_lanes)]

        def piece1(ref, index):
            columns = pl.multiple_of(index * lanes, 128)
            return ref.at[:, pl.ds(columns, lanes)]

        pl.semaphore_wait(barrier, len(friends))
        scatter0, scatter1 = [], []
        for o in range(1, shards):
            where = peer(0, o)
            scatter0.append(send(piece0(part0, where[1]), rs0.at[o], rs_send.at[0, o], rs_recv.at[0, o], where))
            scatter0[-1].start()
        for o in range(1, shards):
            where = peer(0, o)
            scatter1.append(send(piece1(part1, where[1]), rs1.at[o], rs_send.at[1, o], rs_recv.at[1, o], where))
            scatter1[-1].start()

        def first_columns(j, carry):
            columns = pl.ds(pl.multiple_of(j * 128, 128), 128)
            product = lax.dot_general(x[...], w[:, columns], NN, preferred_element_type=F32)
            product = product - t[:, columns].astype(F32)
            first[:, columns] = product
            sums[0, :, columns] = product.astype(BF16)
            return carry

        lax.fori_loop(0, hidden // 128, first_columns, 0)

        for copy in scatter0:
            copy.wait_recv()
        total = piece0(part0, s)[...]
        for o in range(1, shards):
            total = total + rs0[o]
        own0[...] = total
        piece0(p_own, s)[...] = total
        gather0 = []
        for dr, o in [(0, o) for o in range(1, shards)] + [(1, o) for o in range(shards)]:
            target = piece0(p_own if dr == 0 else p_in.at[0], s)
            number = o if dr == 0 else shards + o
            gather0.append(send(own0, target, ag_send.at[number], ag_recv.at[number], peer(dr, o)))
            gather0[-1].start()
        for copy in scatter1:
            copy.wait_recv()
        total = piece1(part1, s)[...]
        for o in range(1, shards):
            total = total + rs1[o]
        own1[...] = total
        piece1(v12, s)[...] = total
        gather1 = []
        for o in range(1, shards):
            number = 2 * shards + o
            gather1.append(send(own1, piece1(v12, s), ag_send.at[number], ag_recv.at[number], peer(0, o)))
            gather1[-1].start()

        def gram_columns(j, carry):
            columns = pl.ds(pl.multiple_of(j * 128, 128), 128)
            gram_x[:, columns] = lax.dot_general(
                x[...], x[columns, :], NT, preferred_element_type=F32
            ).astype(BF16)
            return carry

        lax.fori_loop(0, tokens // 128, gram_columns, 0)

        def next_sum(step):
            def columns_of(j, carry):
                columns = pl.ds(pl.multiple_of(j * 128, 128), 128)
                last = sums[step - 1, :, columns]
                product = lax.dot_general(gram_x[...], last, NN, preferred_element_type=F32)
                sums[step, :, columns] = (first[:, columns] + last.astype(F32) - 0.3 * product).astype(BF16)
                return carry

            lax.fori_loop(0, hidden // 128, columns_of, 0)

        def exchange(source, target, kind, step):
            copy = send(source, target, x_send.at[kind, step], x_recv.at[kind, step], peer(DISTANCES[step], 0))
            copy.start()
            return copy

        for copy in gather0:
            copy.wait_recv()
        basis0 = orthonormal(p_own[...] - p_in[0])
        for copy in gather1:
            copy.wait_recv()
        image, goal = v12[:, :depth], v12[:, depth:]
        inner0 = fine(image, basis0, NT)
        c_out[0, :, :RANK] = inner0
        sent_c0 = exchange(c_out.at[0], c_in.at[0], 0, 0)

        inside0 = lax.dot_general(basis0, x[...], NT, preferred_element_type=F32)
        image = stepped(image, goal)
        moved0 = basis0.astype(F32) - 0.3 * fine(inside0, x[...], NN)
        sent_c0.wait_recv()
        inner0 = inner0 - c_in[0, :, :RANK]
        image = image - 0.5 * lax.dot_general(inner0, moved0, NN, precision=HIGH, preferred_element_type=F32)
        p_in_1 = image[:RANK]
        for copy in scatter0:
            copy.wait_send()
        part0[...] = p_in_1
        sent_p1 = exchange(part0, p_in.at[1], 1, 1)

        right0 = lax.dot_general(basis0, w[...], NN, preferred_element_type=F32)
        right0 = right0 - 0.3 * mm(inside0, sums[0], NN)
        q_out[0] = right0
        sent_q0 = exchange(q_out.at[0], q_in.at[0], 2, 0)
        next_sum(1)

        image, goal = image[RANK:], goal[RANK:]
        sent_p1.wait_recv()
        basis1 = orthonormal(p_in_1 - p_in[1])
        inner1 = fine(image, basis1, NT)
        c_out[1, :RANK, :RANK] = inner1
        sent_c1 = exchange(c_out.at[1], c_in.at[1], 0, 1)
        inside1 = lax.dot_general(basis1, x[...], NT, preferred_element_type=F32)
        image = stepped(image, goal)
        moved1 = basis1.astype(F32) - 0.3 * fine(inside1, x[...], NN)
        sent_c1.wait_recv()
        inner1 = inner1 - c_in[1, :RANK, :RANK]
        image = image - 0.5 * lax.dot_general(inner1, moved1, NN, precision=HIGH, preferred_element_type=F32)
        for copy in gather0:
            copy.wait_send()
        p_own[...] = image
        sent_p2 = exchange(p_own, p_in.at[2], 1, 2)

        sent_q0.wait_recv()
        right0 = right0 - q_in[0]
        right1 = lax.dot_general(basis1, w[...], NN, preferred_element_type=F32)
        right1 = right1 - 0.3 * mm(inside1, sums[1], NN) - 0.5 * mm(mm(basis1, moved0, NT), right0, NN)
        q_out[1] = right1
        sent_q1 = exchange(q_out.at[1], q_in.at[1], 2, 1)
        twice0 = moved0 - 0.3 * fine(fine(moved0, x[...], NT), x[...], NN)
        next_sum(2)

        def grown_rows(j, carry):
            rows = pl.ds(pl.multiple_of(j * 256, 256), 256)
            product = lax.dot_general(x[:, rows], sums[2], TN, preferred_element_type=F32)
            grown[rows, :] = (w[rows, :].astype(F32) - 0.3 * product).astype(BF16)
            return carry

        lax.fori_loop(0, depth // 256, grown_rows, 0)
        written = pltpu.make_async_copy(grown, grown_hbm, load_sem.at[chunks + 2])
        written.start()

        sent_p2.wait_recv()
        basis2 = orthonormal(image - p_in[2])
        sent_q1.wait_recv()
        right1 = right1 - q_in[1]
        right2 = lax.dot_general(basis2, grown[...], NN, preferred_element_type=F32)
        right2 = right2 - 0.5 * mm(mm(basis2, twice0, NT), right0, NN)
        right2 = right2 - 0.5 * mm(mm(basis2, moved1, NT), right1, NN)
        q_out[2] = right2
        sent_q2 = exchange(q_out.at[2], q_in.at[2], 2, 2)
        bases_ref[:RANK, :] = twice0.astype(BF16)
        bases_ref[RANK : 2 * RANK, :] = moved1.astype(BF16)
        bases_ref[2 * RANK :, :] = basis2
        rights_ref[:RANK, :] = right0.astype(BF16)
        rights_ref[RANK : 2 * RANK, :] = right1.astype(BF16)
        for copy in scatter1 + gather1 + [sent_c0, sent_c1, sent_p1, sent_p2, sent_q0, sent_q1]:
            copy.wait_send()
        written.wait()
        sent_q2.wait_recv()
        rights_ref[2 * RANK :, :] = (right2 - q_in[2]).astype(BF16)
        sent_q2.wait_send()

    vm, dma = pltpu.VMEM, pltpu.SemaphoreType.DMA
    scratch = [
        vm((depth, hidden), BF16), vm((tokens, depth), BF16), vm((tokens, hidden), BF16),
        vm((tokens, hidden), F32), vm((3, tokens, hidden), BF16), vm((tokens, tokens), BF16),
        vm((depth, hidden), BF16),
        vm((RANK, depth), F32), vm((2 * RANK, wide), F32),
        vm((shards, 8, part_lanes), F32), vm((shards, 2 * RANK, lanes), F32),
        vm((8, part_lanes), F32), vm((2 * RANK, lanes), F32),
        vm((RANK, depth), F32), vm((3, RANK, depth), F32), vm((2 * RANK, wide), F32),
        vm((2, 2 * RANK, 128), F32), vm((2, 2 * RANK, 128), F32),
        vm((3, RANK, hidden), F32), vm((3, RANK, hidden), F32),
        dma((depth // CHUNK + 3,)), dma((2, shards)), dma((2, shards)),
        dma((3 * shards,)), dma((3 * shards,)), dma((3, 3)), dma((3, 3)),
    ]
    return kernel, scratch


def solution(mesh):
    replicas, shards = mesh.shape["replica"], mesh.shape["shard"]

    def per_device(weights, x, targets, factors):
        weight = weights[0]
        depth, hidden = weight.shape
        tokens = x.shape[0]
        shared = factors.transpose(0, 2, 1).reshape(3 * RANK, hidden)
        kernel, scratch = make_kernel(replicas, shards, depth, hidden, tokens)
        in_vmem = pl.BlockSpec(memory_space=pltpu.VMEM)
        anywhere = pl.BlockSpec(memory_space=pl.ANY)
        grown, bases, rights = pl.pallas_call(
            kernel,
            out_shape=(
                jax.ShapeDtypeStruct((depth, hidden), BF16),
                jax.ShapeDtypeStruct((3 * RANK, depth), BF16),
                jax.ShapeDtypeStruct((3 * RANK, hidden), BF16),
            ),
            in_specs=[anywhere, anywhere, anywhere, in_vmem],
            out_specs=(anywhere, in_vmem, in_vmem),
            scratch_shapes=scratch,
            compiler_params=pltpu.CompilerParams(
                collective_id=0, has_side_effects=True, vmem_limit_bytes=56 * 2**20
            ),
            name="rounds",
        )(weight, x, targets, shared)
        delta = lax.dot_general(bases, rights, TN, preferred_element_type=F32)
        return (grown.astype(F32) - 0.5 * delta).astype(BF16)[None]

    in_specs = (
        P("replica", None, "shard"),
        P("replica", None),
        P("replica", "shard"),
        P(None, "shard", None),
    )
    return jax.shard_map(
        per_device, mesh=mesh, in_specs=in_specs, out_specs=P("replica", None, "shard"), check_vma=False
    )
```

time: 218 us -> 65.9 us (0.30)
  waiting for transfers between devices: 103 us -> 0 us
  Pallas kernels: 0 us -> 59.7 us
  matrix products: 64.7 us -> 6.03 us
  other arithmetic: 17.9 us -> 0 us
  local copies, waits for them, and re-layouts: 17.1 us -> 0 us
  between operations: 13.7 us -> 0.01 us
    psum x1 -> x0, waiting for transfers between devices: 80.1 us -> none  [per_device(): total = lax.psum(partial, 'shard')]
    pallas_call x0 -> x1, Pallas kernels: none -> 59.7 us  [per_device(): pl.pallas_call(kernel, out_shape=(jax.ShapeDtypeStruct((depth, hidden), B...]
    dot_general x32 -> x1, matrix products: 62.7 us -> 6.03 us  [per_device(): delta = lax.dot_general(bases, rights, TN, preferred_element_type=F32)]
    ppermute x8 -> x0, waiting for transfers between devices: 23.2 us -> none  [passed_along(): return lax.ppermute(value, axis, pairs)]
    another operation x18 -> x0, other arithmetic: 15.3 us -> none  [the longest x9 7.34 us: orthonormal(): lower = jnp.linalg.cholesky(gram)]
    unnamed x33 -> x0, local copies, waits for them, and re-layouts: 9.72 us -> none
    broadcast_in_dim x1 -> x0, local copies, waits for them, and re-layouts: 7.17 us -> none  [per_device(): return (grown - 0.5 * low_rank).astype(BF16)[None]]
  transfers between devices with their start and end apart: 9 -> 0, of which waited for: 6 -> 0; matrix products, arithmetic and copies ran while one was open for 17% -> 0% of each run, Pallas kernels for 0% -> 0%
where the time goes in v2:
time: 65.9 us; the launch traced here: 65.7 us
  Pallas kernels  59.7 us (91%)
  matrix products  6.03 us (9%)
    pallas_call x1, Pallas kernels, per_device(): pl.pallas_call(kernel, out_shape=(jax.ShapeDtypeStruct((depth, hidden), B...  59.7 us
    dot_general x1, matrix products, per_device(): delta = lax.dot_general(bases, rights, TN, preferred_element_type=F32)  6.03 us

profile of v2, /device:TPU:0, one launch (start us, length us, event | category | flops | bytes accessed | tf_op | source)
XLA Modules:
  0.0 65.7 jit_solution(9952313650466864808)
XLA Ops:
  0.0 59.7 %rounds.1 = (bf16[2560,896]{1,0:T(8,128)(2,1)}, bf16[48,2560]{1,0:T(8,128)(2,1)}, bf16[48,896]{1,0:T(8,128)(2,1)}) custom-call(bf16[2560,896]{1,0:T(8,128)(2,1)} %bitcast.8, bf16[512,2560]{1,0:T(8,128)(2,1)} %x_hbm.1, bf16[512,896]{1,0:T(8,128)(2,1)} %t_hbm.1, f32[48,896]{1,0:T(8,128)} %bitcast.9), custom_call_target="tpu_custom_call" | custom-call | tf_op jit(solution)/shard_map/rounds/pallas_call | solution.py:313
  59.7 6.0 %fusion = bf16[1,2560,896]{2,1,0:T(8,128)(2,1)} fusion(bf16[48,2560]{1,0:T(8,128)(2,1)} %get-tuple-element.9, bf16[48,896]{1,0:T(8,128)(2,1)} %get-tuple-element.10, bf16[2560,896]{1,0:T(8,128)(2,1)} %get-tuple-element.8), kind=kOutput, calls=%fused_computation.1 | convolution fusion | flops 229376000 | bytes 9506816 | tf_op jit(solution)/shard_map/dot_general | solution.py:328

commit v3 on v2

v3 whole, which is shorter than its diff:
```python
import jax
import jax.numpy as jnp
from jax import lax
from jax.experimental import pallas as pl
from jax.experimental.pallas import tpu as pltpu
from jax.sharding import PartitionSpec as P

RANK = 16
DISTANCES = (1, 2, 4)
F32, BF16 = jnp.float32, jnp.bfloat16
NT = (((1,), (1,)), ((), ()))
NN = (((1,), (0,)), ((), ()))
TN = (((0,), (0,)), ((), ()))
MESH = pl.DeviceIdType.MESH
CHUNK = 512


def mm(a, b, dims):
    return lax.dot_general(a.astype(BF16), b.astype(BF16), dims, preferred_element_type=F32)


def inverse_factor(gram):
    shape = (RANK, 128)
    lane = lax.broadcasted_iota(jnp.int32, shape, 1)
    row = lax.broadcasted_iota(jnp.int32, shape, 0)
    inverse = jnp.where(lane == row, 1.0, 0.0).astype(F32)
    columns = [jnp.broadcast_to(gram[:, k : k + 1], shape) for k in range(RANK)]
    pivots = jnp.ones(shape, F32)
    for j in range(RANK):
        pivot = jnp.broadcast_to(columns[j][j : j + 1, :], shape)
        pivots = jnp.where(row == j, pivot, pivots)
        if j < RANK - 1:
            factor = jnp.where(row > j, columns[j] / pivot, 0.0)
            for k in range(j + 1, RANK):
                columns[k] = columns[k] - factor * jnp.broadcast_to(columns[k][j : j + 1, :], shape)
            inverse = inverse - factor * jnp.broadcast_to(inverse[j : j + 1, :], shape)
    return (lax.rsqrt(pivots) * inverse)[:, :RANK]


def orthonormal(diff):
    high = diff.astype(BF16)
    rest = diff - high.astype(F32)
    middle = rest.astype(BF16)
    low = (rest - middle.astype(F32)).astype(BF16)
    pieces = jnp.concatenate([high, middle, low], axis=0)
    gram = lax.dot_general(pieces, pieces, NT, preferred_element_type=F32)
    gram = gram[:RANK] + gram[RANK : 2 * RANK] + gram[2 * RANK :]
    gram = gram[:, :RANK] + gram[:, RANK : 2 * RANK] + gram[:, 2 * RANK :]
    inverse = inverse_factor(gram)
    top = inverse.astype(BF16)
    inverse = jnp.concatenate([top, (inverse - top.astype(F32)).astype(BF16)], axis=0)
    basis = lax.dot_general(inverse, high, NN, preferred_element_type=F32)
    basis = basis + lax.dot_general(inverse, middle, NN, preferred_element_type=F32)
    return (basis[:RANK] + basis[RANK:]).astype(BF16)


def make_kernel(replicas, shards, depth, hidden, tokens):
    wide = depth + tokens
    lanes = wide // shards
    blocks = [(c, min(256, hidden - c)) for c in range(0, hidden, 256)]

    def kernel(
        w_hbm, x_hbm, t_hbm, f_hbm, grown, bases_ref, rights_ref,
        f, w, x, t, first, sums, gram_x,
        part0, part1, rs0, rs1, own0, own1, p_own, p0_in, p_out, p_in, v12, c_out, c_in, q_out, q_in,
        load_sem, rs_send, rs_recv, ag_send, ag_recv, x_send, x_recv,
    ):
        r, s = lax.axis_index("replica"), lax.axis_index("shard")

        def peer(dr, ds):
            return (lax.rem(r + (dr + replicas), replicas), lax.rem(s + ds, shards))

        def load(source, target, number):
            return pltpu.make_async_copy(source, target, load_sem.at[number])

        def send(source, target, send_sem, recv_sem, where):
            return pltpu.make_async_remote_copy(
                src_ref=source, dst_ref=target, send_sem=send_sem, recv_sem=recv_sem,
                device_id=where, device_id_type=MESH,
            )

        chunks = depth // CHUNK
        loads = [load(f_hbm, f, chunks + 2)]
        loads += [
            load(w_hbm.at[pl.ds(c * CHUNK, CHUNK)], w.at[pl.ds(c * CHUNK, CHUNK)], c)
            for c in range(chunks)
        ]
        loads += [load(t_hbm, t, chunks), load(x_hbm, x, chunks + 1)]
        for copy in loads:
            copy.start()

        barrier = pltpu.get_barrier_semaphore()
        friends = [(0, o) for o in range(1, shards)]
        friends += [(1, o) for o in range(shards)] + [(-1, o) for o in range(shards)]
        friends += [(2, 0), (-2, 0), (4, 0), (-4, 0)]
        for dr, ds in friends:
            pl.semaphore_signal(barrier, inc=1, device_id=peer(dr, ds), device_id_type=MESH)

        c_out[...] = jnp.zeros_like(c_out)
        loads[0].wait()
        shared = f[...].astype(BF16)
        images = []
        for c in range(chunks):
            loads[1 + c].wait()
            images.append(mm(shared, w[c * CHUNK : (c + 1) * CHUNK, :], NT))
        loads[1 + chunks].wait()
        goal = mm(shared, t[...], NT)
        loads[2 + chunks].wait()
        image = jnp.concatenate(images, axis=1)
        image = image - 0.3 * mm(mm(image, x[...], NT) - goal, x[...], NN)
        image, goal = image.astype(BF16), goal.astype(BF16)
        part0[:, :depth] = image[:RANK]
        part0[:, depth:] = goal[:RANK]
        part1[:, :depth] = image[RANK:]
        part1[:, depth:] = goal[RANK:]

        def piece(ref, index):
            return ref.at[:, pl.ds(pl.multiple_of(index * lanes, 128), lanes)]

        pl.semaphore_wait(barrier, len(friends))
        scatter0, scatter1 = [], []
        for o in range(1, shards):
            where = peer(0, o)
            scatter0.append(send(piece(part0, where[1]), rs0.at[o], rs_send.at[0, o], rs_recv.at[0, o], where))
            scatter0[-1].start()
        for o in range(1, shards):
            where = peer(0, o)
            scatter1.append(send(piece(part1, where[1]), rs1.at[o], rs_send.at[1, o], rs_recv.at[1, o], where))
            scatter1[-1].start()

        for c, width in blocks:
            product = mm(x[...], w[:, c : c + width], NN) - t[:, c : c + width].astype(F32)
            first[:, c : c + width] = product
            sums[0, :, c : c + width] = product.astype(BF16)

        for copy in scatter0:
            copy.wait_recv()
        total = piece(part0, s)[...].astype(F32)
        for o in range(1, shards):
            total = total + rs0[o].astype(F32)
        own0[...] = total.astype(BF16)
        piece(p_own, s)[...] = total.astype(BF16)
        gather0 = []
        for dr, o in [(0, o) for o in range(1, shards)] + [(1, o) for o in range(shards)]:
            target = piece(p_own if dr == 0 else p0_in, s)
            number = o if dr == 0 else shards + o
            gather0.append(send(own0, target, ag_send.at[number], ag_recv.at[number], peer(dr, o)))
            gather0[-1].start()
        for copy in scatter1:
            copy.wait_recv()
        total = piece(part1, s)[...].astype(F32)
        for o in range(1, shards):
            total = total + rs1[o].astype(F32)
        own1[...] = total.astype(BF16)
        piece(v12, s)[...] = total.astype(BF16)
        gather1 = []
        for o in range(1, shards):
            number = 2 * shards + o
            gather1.append(send(own1, piece(v12, s), ag_send.at[number], ag_recv.at[number], peer(0, o)))
            gather1[-1].start()

        for c in range(0, tokens, 256):
            gram_x[:, c : c + 256] = mm(x[...], x[c : c + 256, :], NT).astype(BF16)
        for step in (1, 2):
            for c, width in blocks:
                last = sums[step - 1, :, c : c + width]
                product = mm(gram_x[...], last, NN)
                value = first[:, c : c + width] + last.astype(F32) - 0.3 * product
                sums[step, :, c : c + width] = value.astype(BF16)

        def grow(c):
            rows = slice(c * CHUNK, (c + 1) * CHUNK)
            product = mm(x[:, rows], sums[2], TN)
            grown[rows, :] = (w[rows, :].astype(F32) - 0.3 * product).astype(BF16)

        def exchange(source, target, kind, step):
            copy = send(source, target, x_send.at[kind, step], x_recv.at[kind, step], peer(DISTANCES[step], 0))
            copy.start()
            return copy

        for copy in gather0:
            copy.wait_recv()
        basis0 = orthonormal(p_own[:, :depth].astype(F32) - p0_in[:, :depth].astype(F32))
        for copy in gather1:
            copy.wait_recv()
        image = v12[:, :depth]
        inner0 = mm(image, basis0, NT)
        c_out[0, :, :RANK] = inner0
        sent_c0 = exchange(c_out.at[0], c_in.at[0], 0, 0)
        inside = mm(jnp.concatenate([image, basis0], axis=0), x[...], NT)
        inside0 = inside[2 * RANK :]
        inside = jnp.concatenate([inside[: 2 * RANK] - v12[:, depth:].astype(F32), inside0], axis=0)
        change = 0.3 * mm(inside, x[...], NN)
        image = image.astype(F32) - change[: 2 * RANK]
        moved0 = basis0.astype(F32) - change[2 * RANK :]
        sent_c0.wait_recv()
        inner0 = inner0 - c_in[0, :, :RANK]
        image = image - 0.5 * mm(inner0, moved0, NN)
        left1 = image[:RANK]
        p_out[0] = left1.astype(BF16)
        sent_p1 = exchange(p_out.at[0], p_in.at[0], 1, 1)

        right0 = mm(basis0, w[...], NN) - 0.3 * mm(inside0, sums[0], NN)
        q_out[0] = right0.astype(BF16)
        sent_q0 = exchange(q_out.at[0], q_in.at[0], 2, 0)
        image = image[RANK:]
        inside = mm(jnp.concatenate([image, moved0], axis=0), x[...], NT)
        inside = jnp.concatenate([inside[:RANK] - v12[RANK:, depth:].astype(F32), inside[RANK:]], axis=0)
        change = 0.3 * mm(inside, x[...], NN)
        next_image = image - change[:RANK]
        twice0 = moved0 - change[RANK:]
        grow(0)
        grow(1)

        sent_p1.wait_recv()
        basis1 = orthonormal(left1 - p_in[0].astype(F32))
        inner1 = mm(image, basis1, NT)
        c_out[1, :RANK, :RANK] = inner1
        sent_c1 = exchange(c_out.at[1], c_in.at[1], 0, 1)
        inside1 = mm(basis1, x[...], NT)
        moved1 = basis1.astype(F32) - 0.3 * mm(inside1, x[...], NN)
        sent_c1.wait_recv()
        inner1 = inner1 - c_in[1, :RANK, :RANK]
        left2 = next_image - 0.5 * mm(inner1, moved1, NN)
        p_out[1] = left2.astype(BF16)
        sent_p2 = exchange(p_out.at[1], p_in.at[1], 1, 2)

        sent_q0.wait_recv()
        right0 = right0 - q_in[0].astype(F32)
        right1 = mm(basis1, w[...], NN) - 0.3 * mm(inside1, sums[1], NN)
        right1 = right1 - 0.5 * mm(mm(basis1, moved0, NT), right0, NN)
        q_out[1] = right1.astype(BF16)
        sent_q1 = exchange(q_out.at[1], q_in.at[1], 2, 1)
        for c in range(2, chunks):
            grow(c)
        bases_ref[:RANK, :] = twice0.astype(BF16)
        bases_ref[RANK : 2 * RANK, :] = moved1.astype(BF16)
        rights_ref[:RANK, :] = right0.astype(BF16)

        sent_p2.wait_recv()
        basis2 = orthonormal(left2 - p_in[1].astype(F32))
        sent_q1.wait_recv()
        right1 = right1 - q_in[1].astype(F32)
        right2 = mm(basis2, grown[...], NN)
        right2 = right2 - 0.5 * mm(mm(basis2, twice0, NT), right0, NN)
        right2 = right2 - 0.5 * mm(mm(basis2, moved1, NT), right1, NN)
        q_out[2] = right2.astype(BF16)
        sent_q2 = exchange(q_out.at[2], q_in.at[2], 2, 2)
        bases_ref[2 * RANK :, :] = basis2
        rights_ref[RANK : 2 * RANK, :] = right1.astype(BF16)
        started = scatter0 + scatter1 + gather0 + gather1
        for copy in started + [sent_c0, sent_c1, sent_p1, sent_p2, sent_q0, sent_q1]:
            copy.wait_send()
        sent_q2.wait_recv()
        rights_ref[2 * RANK :, :] = (right2 - q_in[2].astype(F32)).astype(BF16)
        sent_q2.wait_send()

    vm, dma = pltpu.VMEM, pltpu.SemaphoreType.DMA
    scratch = [
        vm((3 * RANK, hidden), F32), vm((depth, hidden), BF16), vm((tokens, depth), BF16), vm((tokens, hidden), BF16),
        vm((tokens, hidden), F32), vm((3, tokens, hidden), BF16), vm((tokens, tokens), BF16),
        vm((RANK, wide), BF16), vm((2 * RANK, wide), BF16),
        vm((shards, RANK, lanes), BF16), vm((shards, 2 * RANK, lanes), BF16),
        vm((RANK, lanes), BF16), vm((2 * RANK, lanes), BF16),
        vm((RANK, wide), BF16), vm((RANK, wide), BF16), vm((2, RANK, depth), BF16), vm((2, RANK, depth), BF16),
        vm((2 * RANK, wide), BF16),
        vm((2, 2 * RANK, 128), F32), vm((2, 2 * RANK, 128), F32),
        vm((3, RANK, hidden), BF16), vm((3, RANK, hidden), BF16),
        dma((depth // CHUNK + 3,)), dma((2, shards)), dma((2, shards)),
        dma((3 * shards,)), dma((3 * shards,)), dma((3, 3)), dma((3, 3)),
    ]
    return kernel, scratch


def solution(mesh):
    replicas, shards = mesh.shape["replica"], mesh.shape["shard"]

    def per_device(weights, x, targets, factors):
        weight = weights[0]
        depth, hidden = weight.shape
        tokens = x.shape[0]
        shared = factors.transpose(0, 2, 1).reshape(3 * RANK, hidden)
        kernel, scratch = make_kernel(replicas, shards, depth, hidden, tokens)
        in_vmem = pl.BlockSpec(memory_space=pltpu.VMEM)
        grown, bases, rights = pl.pallas_call(
            kernel,
            out_shape=(
                pltpu.VMEM((depth, hidden), BF16),
                jax.ShapeDtypeStruct((3 * RANK, depth), BF16),
                jax.ShapeDtypeStruct((3 * RANK, hidden), BF16),
            ),
            in_specs=[pl.BlockSpec(memory_space=pltpu.HBM)] * 4,
            out_specs=(in_vmem, in_vmem, in_vmem),
            scratch_shapes=scratch,
            compiler_params=pltpu.CompilerParams(
                collective_id=0, has_side_effects=True, vmem_limit_bytes=40 * 2**20
            ),
            name="rounds",
        )(*(pltpu.with_memory_space_constraint(v, pltpu.HBM) for v in (weight, x, targets, shared)))
        delta = lax.dot_general(bases, rights, TN, preferred_element_type=F32)
        return (grown.astype(F32) - 0.5 * delta).astype(BF16)[None]

    in_specs = (
        P("replica", None, "shard"),
        P("replica", None),
        P("replica", "shard"),
        P(None, "shard", None),
    )
    return jax.shard_map(
        per_device, mesh=mesh, in_specs=in_specs, out_specs=P("replica", None, "shard"), check_vma=False
    )
```

time: 65.9 us -> 46.7 us (0.71)
  Pallas kernels: 59.7 us -> 43.1 us
  matrix products: 6.03 us -> 3.54 us
    pallas_call x1, Pallas kernels: 59.7 us -> 43.1 us  [per_device(): pl.pallas_call(kernel, out_shape=(pltpu.VMEM((depth, hidden), BF16), jax....]
    dot_general x1, matrix products: 6.03 us -> 3.54 us  [per_device(): delta = lax.dot_general(bases, rights, TN, preferred_element_type=F32)]
where the time goes in v3:
time: 46.7 us; the launch traced here: 46.6 us
  Pallas kernels  43.1 us (92%)
  matrix products  3.54 us (8%)
    pallas_call x1, Pallas kernels, per_device(): pl.pallas_call(kernel, out_shape=(pltpu.VMEM((depth, hidden), BF16), jax....  43.1 us
    dot_general x1, matrix products, per_device(): delta = lax.dot_general(bases, rights, TN, preferred_element_type=F32)  3.54 us

profile of v3, /device:TPU:0, one launch (start us, length us, event | category | flops | bytes accessed | tf_op | source)
XLA Modules:
  0.0 46.6 jit_solution(17234656829819470642)
XLA Ops:
  0.0 43.1 %rounds.1 = (bf16[2560,896]{1,0:T(8,128)(2,1)S(1)}, bf16[48,2560]{1,0:T(8,128)(2,1)S(1)}, bf16[48,896]{1,0:T(8,128)(2,1)S(1)}) custom-call(bf16[2560,896]{1,0:T(8,128)(2,1)} %bitcast.8, bf16[512,2560]{1,0:T(8,128)(2,1)} %x_hbm.1, bf16[512,896]{1,0:T(8,128)(2,1)} %t_hbm.1, f32[48,896]{1,0:T(8,128)} %bitcast.9), custom_call_target="tpu_custom_call" | custom-call | tf_op jit(solution)/shard_map/rounds/pallas_call | solution.py:285
  43.1 3.5 %fusion = bf16[1,2560,896]{2,1,0:T(8,128)(2,1)} fusion(bf16[48,2560]{1,0:T(8,128)(2,1)S(1)} %get-tuple-element.9, bf16[48,896]{1,0:T(8,128)(2,1)S(1)} %get-tuple-element.10, bf16[2560,896]{1,0:T(8,128)(2,1)S(1)} %get-tuple-element.8), kind=kOutput, calls=%fused_computation.1 | convolution fusion | flops 229376000 | bytes 9506816 | tf_op jit(solution)/shard_map/dot_general | solution.py:300

commit v4 on v3

--- a/solution.py
+++ b/solution.py
@@ -6,7 +6,6 @@
 from jax.sharding import PartitionSpec as P
 
 RANK = 16
-DISTANCES = (1, 2, 4)
 F32, BF16 = jnp.float32, jnp.bfloat16
 NT = (((1,), (1,)), ((), ()))
 NN = (((1,), (0,)), ((), ()))
@@ -37,7 +36,14 @@
     return (lax.rsqrt(pivots) * inverse)[:, :RANK]
 
 
-def orthonormal(diff):
+def product_of(inverse, value):
+    high = value.astype(BF16)
+    rest = (value - high.astype(F32)).astype(BF16)
+    result = mm(inverse, high, NN) + mm(inverse, rest, NN)
+    return result[:RANK] + result[RANK:]
+
+
+def factored(diff):
     high = diff.astype(BF16)
     rest = diff - high.astype(F32)
     middle = rest.astype(BF16)
@@ -49,9 +55,24 @@
     inverse = inverse_factor(gram)
     top = inverse.astype(BF16)
     inverse = jnp.concatenate([top, (inverse - top.astype(F32)).astype(BF16)], axis=0)
-    basis = lax.dot_general(inverse, high, NN, preferred_element_type=F32)
-    basis = basis + lax.dot_general(inverse, middle, NN, preferred_element_type=F32)
-    return (basis[:RANK] + basis[RANK:]).astype(BF16)
+    return inverse, pieces[: 2 * RANK]
+
+
+def orthonormal(diff):
+    inverse, _ = factored(diff)
+    return product_of(inverse, diff).astype(BF16)
+
+
+def update_kernel(grown, bases, rights, out_hbm, staged, sem):
+    copies = []
+    for number, c in enumerate(range(0, grown.shape[1], 256)):
+        columns = pl.ds(c, min(256, grown.shape[1] - c))
+        delta = mm(bases[...], rights[:, columns], TN)
+        staged[:, columns] = (grown[:, columns].astype(F32) - 0.5 * delta).astype(BF16)
+        copies.append(pltpu.make_async_copy(staged.at[:, columns], out_hbm.at[:, columns], sem.at[number]))
+        copies[-1].start()
+    for copy in copies:
+        copy.wait()
 
 
 def make_kernel(replicas, shards, depth, hidden, tokens):
@@ -80,34 +101,38 @@
             )
 
         chunks = depth // CHUNK
-        loads = [load(f_hbm, f, chunks + 2)]
-        loads += [
-            load(w_hbm.at[pl.ds(c * CHUNK, CHUNK)], w.at[pl.ds(c * CHUNK, CHUNK)], c)
-            for c in range(chunks)
-        ]
-        loads += [load(t_hbm, t, chunks), load(x_hbm, x, chunks + 1)]
+        parts = [(c * CHUNK, CHUNK) for c in range(chunks - 1)]
+        parts += [(depth - CHUNK, CHUNK // 2), (depth - CHUNK // 2, CHUNK // 2)]
+        load_f, load_t = load(f_hbm, f, 0), load(t_hbm, t, 1)
+        load_f.start()
+        load_t.start()
+        loads = []
+        for number, (start, size) in enumerate(parts):
+            span = pl.ds(start, size)
+            loads.append(load(w_hbm.at[span], w.at[span], 2 + 2 * number))
+            loads.append(load(x_hbm.at[:, span], x.at[:, span], 3 + 2 * number))
         for copy in loads:
             copy.start()
 
         barrier = pltpu.get_barrier_semaphore()
         friends = [(0, o) for o in range(1, shards)]
         friends += [(1, o) for o in range(shards)] + [(-1, o) for o in range(shards)]
-        friends += [(2, 0), (-2, 0), (4, 0), (-4, 0)]
+        friends += [(2, 0), (-2, 0), (4, 0), (-4, 0), (6, 0), (-6, 0)]
         for dr, ds in friends:
             pl.semaphore_signal(barrier, inc=1, device_id=peer(dr, ds), device_id_type=MESH)
 
         c_out[...] = jnp.zeros_like(c_out)
-        loads[0].wait()
+        load_f.wait()
         shared = f[...].astype(BF16)
-        images = []
-        for c in range(chunks):
-            loads[1 + c].wait()
-            images.append(mm(shared, w[c * CHUNK : (c + 1) * CHUNK, :], NT))
-        loads[1 + chunks].wait()
+        load_t.wait()
         goal = mm(shared, t[...], NT)
-        loads[2 + chunks].wait()
-        image = jnp.concatenate(images, axis=1)
-        image = image - 0.3 * mm(mm(image, x[...], NT) - goal, x[...], NN)
+        images, inside = [], -goal
+        for number, (start, size) in enumerate(parts):
+            loads[2 * number].wait()
+            images.append(mm(shared, w[start : start + size, :], NT))
+            loads[2 * number + 1].wait()
+            inside = inside + mm(images[-1], x[:, start : start + size], NT)
+        image = jnp.concatenate(images, axis=1) - 0.3 * mm(inside, x[...], NN)
         image, goal = image.astype(BF16), goal.astype(BF16)
         part0[:, :depth] = image[:RANK]
         part0[:, depth:] = goal[:RANK]
@@ -173,8 +198,8 @@
             product = mm(x[:, rows], sums[2], TN)
             grown[rows, :] = (w[rows, :].astype(F32) - 0.3 * product).astype(BF16)
 
-        def exchange(source, target, kind, step):
-            copy = send(source, target, x_send.at[kind, step], x_recv.at[kind, step], peer(DISTANCES[step], 0))
+        def exchange(source, target, number, distance):
+            copy = send(source, target, x_send.at[number], x_recv.at[number], peer(distance, 0))
             copy.start()
             return copy
 
@@ -186,7 +211,7 @@
         image = v12[:, :depth]
         inner0 = mm(image, basis0, NT)
         c_out[0, :, :RANK] = inner0
-        sent_c0 = exchange(c_out.at[0], c_in.at[0], 0, 0)
+        sent_c0 = exchange(c_out.at[0], c_in.at[0], 0, 1)
         inside = mm(jnp.concatenate([image, basis0], axis=0), x[...], NT)
         inside0 = inside[2 * RANK :]
         inside = jnp.concatenate([inside[: 2 * RANK] - v12[:, depth:].astype(F32), inside0], axis=0)
@@ -198,16 +223,18 @@
         image = image - 0.5 * mm(inner0, moved0, NN)
         left1 = image[:RANK]
         p_out[0] = left1.astype(BF16)
-        sent_p1 = exchange(p_out.at[0], p_in.at[0], 1, 1)
+        sent_p1 = exchange(p_out.at[0], p_in.at[0], 1, 2)
 
         right0 = mm(basis0, w[...], NN) - 0.3 * mm(inside0, sums[0], NN)
         q_out[0] = right0.astype(BF16)
-        sent_q0 = exchange(q_out.at[0], q_in.at[0], 2, 0)
+        sent_q0 = exchange(q_out.at[0], q_in.at[0], 2, 1)
         image = image[RANK:]
         inside = mm(jnp.concatenate([image, moved0], axis=0), x[...], NT)
         inside = jnp.concatenate([inside[:RANK] - v12[RANK:, depth:].astype(F32), inside[RANK:]], axis=0)
         change = 0.3 * mm(inside, x[...], NN)
         next_image = image - change[:RANK]
+        p_out[1] = next_image.astype(BF16)
+        sent_p2 = exchange(p_out.at[1], p_in.at[1], 3, 4)
         twice0 = moved0 - change[RANK:]
         grow(0)
         grow(1)
@@ -216,21 +243,21 @@
         basis1 = orthonormal(left1 - p_in[0].astype(F32))
         inner1 = mm(image, basis1, NT)
         c_out[1, :RANK, :RANK] = inner1
-        sent_c1 = exchange(c_out.at[1], c_in.at[1], 0, 1)
+        sent_c1 = [
+            exchange(c_out.at[1, pl.ds(0, RANK)], c_in.at[1 + n, pl.ds(0, RANK)], 4 + n, distance)
+            for n, distance in enumerate((2, 4, 6))
+        ]
         inside1 = mm(basis1, x[...], NT)
         moved1 = basis1.astype(F32) - 0.3 * mm(inside1, x[...], NN)
-        sent_c1.wait_recv()
-        inner1 = inner1 - c_in[1, :RANK, :RANK]
-        left2 = next_image - 0.5 * mm(inner1, moved1, NN)
-        p_out[1] = left2.astype(BF16)
-        sent_p2 = exchange(p_out.at[1], p_in.at[1], 1, 2)
+        p_out[2] = moved1.astype(BF16)
+        sent_m1 = exchange(p_out.at[2], p_in.at[2], 7, 4)
 
         sent_q0.wait_recv()
         right0 = right0 - q_in[0].astype(F32)
         right1 = mm(basis1, w[...], NN) - 0.3 * mm(inside1, sums[1], NN)
         right1 = right1 - 0.5 * mm(mm(basis1, moved0, NT), right0, NN)
         q_out[1] = right1.astype(BF16)
-        sent_q1 = exchange(q_out.at[1], q_in.at[1], 2, 1)
+        sent_q1 = exchange(q_out.at[1], q_in.at[1], 8, 2)
         for c in range(2, chunks):
             grow(c)
         bases_ref[:RANK, :] = twice0.astype(BF16)
@@ -238,18 +265,26 @@
         rights_ref[:RANK, :] = right0.astype(BF16)
 
         sent_p2.wait_recv()
-        basis2 = orthonormal(left2 - p_in[1].astype(F32))
+        for copy in sent_c1:
+            copy.wait_recv()
+        inner = inner1 - c_in[1, :RANK, :RANK]
+        left2 = next_image - 0.5 * mm(inner, moved1, NN)
+        inner = c_in[2, :RANK, :RANK] - c_in[3, :RANK, :RANK]
         sent_q1.wait_recv()
         right1 = right1 - q_in[1].astype(F32)
-        right2 = mm(basis2, grown[...], NN)
-        right2 = right2 - 0.5 * mm(mm(basis2, twice0, NT), right0, NN)
-        right2 = right2 - 0.5 * mm(mm(basis2, moved1, NT), right1, NN)
+        sent_m1.wait_recv()
+        left2 = left2 - (p_in[1].astype(F32) - 0.5 * mm(inner, p_in[2], NN))
+        inverse, pieces = factored(left2)
+        raw = mm(pieces, grown[...], NN)
+        raw = raw - 0.5 * mm(mm(pieces, twice0, NT), right0, NN) - 0.5 * mm(mm(pieces, moved1, NT), right1, NN)
+        right2 = product_of(inverse, raw[:RANK] + raw[RANK:])
         q_out[2] = right2.astype(BF16)
-        sent_q2 = exchange(q_out.at[2], q_in.at[2], 2, 2)
+        sent_q2 = exchange(q_out.at[2], q_in.at[2], 9, 4)
+        basis2 = product_of(inverse, left2).astype(BF16)
         bases_ref[2 * RANK :, :] = basis2
         rights_ref[RANK : 2 * RANK, :] = right1.astype(BF16)
         started = scatter0 + scatter1 + gather0 + gather1
-        for copy in started + [sent_c0, sent_c1, sent_p1, sent_p2, sent_q0, sent_q1]:
+        for copy in started + sent_c1 + [sent_c0, sent_p1, sent_p2, sent_m1, sent_q0, sent_q1]:
             copy.wait_send()
         sent_q2.wait_recv()
         rights_ref[2 * RANK :, :] = (right2 - q_in[2].astype(F32)).astype(BF16)
@@ -262,12 +297,12 @@
         vm((RANK, wide), BF16), vm((2 * RANK, wide), BF16),
         vm((shards, RANK, lanes), BF16), vm((shards, 2 * RANK, lanes), BF16),
         vm((RANK, lanes), BF16), vm((2 * RANK, lanes), BF16),
-        vm((RANK, wide), BF16), vm((RANK, wide), BF16), vm((2, RANK, depth), BF16), vm((2, RANK, depth), BF16),
+        vm((RANK, wide), BF16), vm((RANK, wide), BF16), vm((3, RANK, depth), BF16), vm((3, RANK, depth), BF16),
         vm((2 * RANK, wide), BF16),
-        vm((2, 2 * RANK, 128), F32), vm((2, 2 * RANK, 128), F32),
+        vm((2, 2 * RANK, 128), F32), vm((4, 2 * RANK, 128), F32),
         vm((3, RANK, hidden), BF16), vm((3, RANK, hidden), BF16),
-        dma((depth // CHUNK + 3,)), dma((2, shards)), dma((2, shards)),
-        dma((3 * shards,)), dma((3 * shards,)), dma((3, 3)), dma((3, 3)),
+        dma((2 * depth // CHUNK + 4,)), dma((2, shards)), dma((2, shards)),
+        dma((3 * shards,)), dma((3 * shards,)), dma((10,)), dma((10,)),
     ]
     return kernel, scratch
 
@@ -297,8 +332,15 @@
             ),
             name="rounds",
         )(*(pltpu.with_memory_space_constraint(v, pltpu.HBM) for v in (weight, x, targets, shared)))
-        delta = lax.dot_general(bases, rights, TN, preferred_element_type=F32)
-        return (grown.astype(F32) - 0.5 * delta).astype(BF16)[None]
+        return pl.pallas_call(
+            update_kernel,
+            out_shape=jax.ShapeDtypeStruct((depth, hidden), BF16),
+            in_specs=[in_vmem] * 3,
+            out_specs=pl.BlockSpec(memory_space=pltpu.HBM),
+            scratch_shapes=[pltpu.VMEM((depth, hidden), BF16), pltpu.SemaphoreType.DMA((pl.cdiv(hidden, 256),))],
+            compiler_params=pltpu.CompilerParams(vmem_limit_bytes=16 * 2**20),
+            name="update",
+        )(grown, bases, rights)[None]
 
     in_specs = (
         P("replica", None, "shard"),

time: 46.7 us -> 45.6 us (0.976)
  matrix products: 3.54 us -> 0 us
  Pallas kernels: 43.1 us -> 45.3 us
    dot_general x1 -> x0, matrix products: 3.54 us -> none  [per_device(): delta = lax.dot_general(bases, rights, TN, preferred_element_type=F32)]
    pallas_call x0 -> x1, Pallas kernels: none -> 2.9 us  [per_device(): pl.pallas_call(update_kernel, out_shape=jax.ShapeDtypeStruct((depth, hidd...]
    pallas_call x1, Pallas kernels: 43.1 us -> 42.4 us  [per_device(): pl.pallas_call(kernel, out_shape=(pltpu.VMEM((depth, hidden), BF16), jax....]
where the time goes in v4:
time: 45.6 us; the launch traced here: 45.5 us
  Pallas kernels  45.3 us (99%)
    pallas_call x1, Pallas kernels, per_device(): pl.pallas_call(kernel, out_shape=(pltpu.VMEM((depth, hidden), BF16), jax....  42.4 us
    pallas_call x1, Pallas kernels, per_device(): pl.pallas_call(update_kernel, out_shape=jax.ShapeDtypeStruct((depth, hidd...  2.9 us

profile of v4, /device:TPU:0, one launch (start us, length us, event | category | flops | bytes accessed | tf_op | source)
XLA Modules:
  0.0 45.5 jit_solution(15946454808575337670)
XLA Ops:
  0.0 42.4 %rounds.1 = (bf16[2560,896]{1,0:T(8,128)(2,1)S(1)}, bf16[48,2560]{1,0:T(8,128)(2,1)S(1)}, bf16[48,896]{1,0:T(8,128)(2,1)S(1)}) custom-call(bf16[2560,896]{1,0:T(8,128)(2,1)} %bitcast.5, bf16[512,2560]{1,0:T(8,128)(2,1)} %x_hbm.1, bf16[512,896]{1,0:T(8,128)(2,1)} %t_hbm.1, f32[48,896]{1,0:T(8,128)} %bitcast.6), custom_call_target="tpu_custom_call" | custom-call | tf_op jit(solution)/shard_map/rounds/pallas_call | solution.py:320
  42.4 2.9 %update.1 = bf16[2560,896]{1,0:T(8,128)(2,1)} custom-call(bf16[2560,896]{1,0:T(8,128)(2,1)S(1)} %get-tuple-element.8.grown, bf16[48,2560]{1,0:T(8,128)(2,1)S(1)} %get-tuple-element.9.bases, bf16[48,896]{1,0:T(8,128)(2,1)S(1)} %get-tuple-element.10.rights), custom_call_target="tpu_custom_call" | custom-call | tf_op jit(solution)/shard_map/update/pallas_call | solution.py:335

commit v5 on v4

--- a/solution.py
+++ b/solution.py
@@ -64,15 +64,13 @@
 
 
 def update_kernel(grown, bases, rights, out_hbm, staged, sem):
-    copies = []
-    for number, c in enumerate(range(0, grown.shape[1], 256)):
+    for c in range(0, grown.shape[1], 256):
         columns = pl.ds(c, min(256, grown.shape[1] - c))
         delta = mm(bases[...], rights[:, columns], TN)
         staged[:, columns] = (grown[:, columns].astype(F32) - 0.5 * delta).astype(BF16)
-        copies.append(pltpu.make_async_copy(staged.at[:, columns], out_hbm.at[:, columns], sem.at[number]))
-        copies[-1].start()
-    for copy in copies:
-        copy.wait()
+    copy = pltpu.make_async_copy(staged, out_hbm, sem)
+    copy.start()
+    copy.wait()
 
 
 def make_kernel(replicas, shards, depth, hidden, tokens):
@@ -101,38 +99,41 @@
             )
 
         chunks = depth // CHUNK
-        parts = [(c * CHUNK, CHUNK) for c in range(chunks - 1)]
-        parts += [(depth - CHUNK, CHUNK // 2), (depth - CHUNK // 2, CHUNK // 2)]
-        load_f, load_t = load(f_hbm, f, 0), load(t_hbm, t, 1)
-        load_f.start()
-        load_t.start()
-        loads = []
-        for number, (start, size) in enumerate(parts):
-            span = pl.ds(start, size)
-            loads.append(load(w_hbm.at[span], w.at[span], 2 + 2 * number))
-            loads.append(load(x_hbm.at[:, span], x.at[:, span], 3 + 2 * number))
-        for copy in loads:
+        halves = [(0, tokens // 2), (tokens // 2, tokens // 2)]
+        load_f = load(f_hbm, f, 0)
+        load_w = [
+            load(w_hbm.at[pl.ds(c * CHUNK, CHUNK)], w.at[pl.ds(c * CHUNK, CHUNK)], 4 + c)
+            for c in range(chunks)
+        ]
+        load_t = load(t_hbm, t, 1)
+        load_x = [load(x_hbm.at[pl.ds(*half)], x.at[pl.ds(*half)], 2 + n) for n, half in enumerate(halves)]
+        for copy in [load_f] + load_w + [load_t] + load_x:
             copy.start()
 
         barrier = pltpu.get_barrier_semaphore()
         friends = [(0, o) for o in range(1, shards)]
         friends += [(1, o) for o in range(shards)] + [(-1, o) for o in range(shards)]
-        friends += [(2, 0), (-2, 0), (4, 0), (-4, 0), (6, 0), (-6, 0)]
+        friends += [(2, 0), (-2, 0), (4, 0), (-4, 0), (6, 0), (-6, 0), (3, 0), (-3, 0)]
         for dr, ds in friends:
             pl.semaphore_signal(barrier, inc=1, device_id=peer(dr, ds), device_id_type=MESH)
 
         c_out[...] = jnp.zeros_like(c_out)
         load_f.wait()
         shared = f[...].astype(BF16)
+        images = []
+        for c in range(chunks):
+            load_w[c].wait()
+            images.append(mm(shared, w[c * CHUNK : (c + 1) * CHUNK, :], NT))
+        image = jnp.concatenate(images, axis=1)
         load_t.wait()
         goal = mm(shared, t[...], NT)
-        images, inside = [], -goal
-        for number, (start, size) in enumerate(parts):
-            loads[2 * number].wait()
-            images.append(mm(shared, w[start : start + size, :], NT))
-            loads[2 * number + 1].wait()
-            inside = inside + mm(images[-1], x[:, start : start + size], NT)
-        image = jnp.concatenate(images, axis=1) - 0.3 * mm(inside, x[...], NN)
+        change = jnp.zeros_like(image)
+        for n, (start, size) in enumerate(halves):
+            load_x[n].wait()
+            rows = slice(start, start + size)
+            inside = mm(image, x[rows, :], NT) - goal[:, rows]
+            change = change + mm(inside, x[rows, :], NN)
+        image = image - 0.3 * change
         image, goal = image.astype(BF16), goal.astype(BF16)
         part0[:, :depth] = image[:RANK]
         part0[:, depth:] = goal[:RANK]
@@ -211,53 +212,58 @@
         image = v12[:, :depth]
         inner0 = mm(image, basis0, NT)
         c_out[0, :, :RANK] = inner0
-        sent_c0 = exchange(c_out.at[0], c_in.at[0], 0, 1)
+        sent_c0 = [exchange(c_out.at[0], c_in.at[n], n, n + 1) for n in range(3)]
         inside = mm(jnp.concatenate([image, basis0], axis=0), x[...], NT)
         inside0 = inside[2 * RANK :]
         inside = jnp.concatenate([inside[: 2 * RANK] - v12[:, depth:].astype(F32), inside0], axis=0)
         change = 0.3 * mm(inside, x[...], NN)
         image = image.astype(F32) - change[: 2 * RANK]
         moved0 = basis0.astype(F32) - change[2 * RANK :]
-        sent_c0.wait_recv()
-        inner0 = inner0 - c_in[0, :, :RANK]
-        image = image - 0.5 * mm(inner0, moved0, NN)
-        left1 = image[:RANK]
-        p_out[0] = left1.astype(BF16)
-        sent_p1 = exchange(p_out.at[0], p_in.at[0], 1, 2)
-
+        p_out[0] = image[:RANK].astype(BF16)
+        p_out[1] = moved0.astype(BF16)
+        sent_p1 = exchange(p_out.at[0], p_in.at[0], 3, 2)
+        sent_m0 = exchange(p_out.at[1], p_in.at[1], 4, 2)
+
+        inside = mm(jnp.concatenate([image[RANK:], moved0], axis=0), x[...], NT)
+        inside = jnp.concatenate([inside[:RANK] - v12[RANK:, depth:].astype(F32), inside[RANK:]], axis=0)
+        change = 0.3 * mm(inside, x[...], NN)
+        next_image = image[RANK:] - change[:RANK]
+        twice0 = moved0 - change[RANK:]
         right0 = mm(basis0, w[...], NN) - 0.3 * mm(inside0, sums[0], NN)
         q_out[0] = right0.astype(BF16)
-        sent_q0 = exchange(q_out.at[0], q_in.at[0], 2, 1)
-        image = image[RANK:]
-        inside = mm(jnp.concatenate([image, moved0], axis=0), x[...], NT)
-        inside = jnp.concatenate([inside[:RANK] - v12[RANK:, depth:].astype(F32), inside[RANK:]], axis=0)
-        change = 0.3 * mm(inside, x[...], NN)
-        next_image = image - change[:RANK]
-        p_out[1] = next_image.astype(BF16)
-        sent_p2 = exchange(p_out.at[1], p_in.at[1], 3, 4)
-        twice0 = moved0 - change[RANK:]
+        sent_q0 = exchange(q_out.at[0], q_in.at[0], 5, 1)
         grow(0)
         grow(1)
 
+        for copy in sent_c0:
+            copy.wait_recv()
+        inner = inner0 - c_in[0, :, :RANK]
+        other = c_in[1, :RANK, :RANK] - c_in[2, :RANK, :RANK]
+        next_image = next_image - 0.5 * mm(inner[RANK:], twice0, NN)
+        p_out[2] = next_image.astype(BF16)
+        sent_p2 = exchange(p_out.at[2], p_in.at[2], 6, 4)
+        image = image - 0.5 * mm(inner, moved0, NN)
+        left1, image = image[:RANK], image[RANK:]
         sent_p1.wait_recv()
-        basis1 = orthonormal(left1 - p_in[0].astype(F32))
+        sent_m0.wait_recv()
+        basis1 = orthonormal(left1 - (p_in[0].astype(F32) - 0.5 * mm(other, p_in[1], NN)))
         inner1 = mm(image, basis1, NT)
         c_out[1, :RANK, :RANK] = inner1
         sent_c1 = [
-            exchange(c_out.at[1, pl.ds(0, RANK)], c_in.at[1 + n, pl.ds(0, RANK)], 4 + n, distance)
+            exchange(c_out.at[1, pl.ds(0, RANK)], c_in.at[3 + n, pl.ds(0, RANK)], 7 + n, distance)
             for n, distance in enumerate((2, 4, 6))
         ]
         inside1 = mm(basis1, x[...], NT)
         moved1 = basis1.astype(F32) - 0.3 * mm(inside1, x[...], NN)
-        p_out[2] = moved1.astype(BF16)
-        sent_m1 = exchange(p_out.at[2], p_in.at[2], 7, 4)
+        p_out[3] = moved1.astype(BF16)
+        sent_m1 = exchange(p_out.at[3], p_in.at[3], 10, 4)
 
         sent_q0.wait_recv()
         right0 = right0 - q_in[0].astype(F32)
         right1 = mm(basis1, w[...], NN) - 0.3 * mm(inside1, sums[1], NN)
         right1 = right1 - 0.5 * mm(mm(basis1, moved0, NT), right0, NN)
         q_out[1] = right1.astype(BF16)
-        sent_q1 = exchange(q_out.at[1], q_in.at[1], 8, 2)
+        sent_q1 = exchange(q_out.at[1], q_in.at[1], 11, 2)
         for c in range(2, chunks):
             grow(c)
         bases_ref[:RANK, :] = twice0.astype(BF16)
@@ -267,27 +273,36 @@
         sent_p2.wait_recv()
         for copy in sent_c1:
             copy.wait_recv()
-        inner = inner1 - c_in[1, :RANK, :RANK]
+        inner = inner1 - c_in[3, :RANK, :RANK]
         left2 = next_image - 0.5 * mm(inner, moved1, NN)
-        inner = c_in[2, :RANK, :RANK] - c_in[3, :RANK, :RANK]
+        other = c_in[4, :RANK, :RANK] - c_in[5, :RANK, :RANK]
         sent_q1.wait_recv()
         right1 = right1 - q_in[1].astype(F32)
         sent_m1.wait_recv()
-        left2 = left2 - (p_in[1].astype(F32) - 0.5 * mm(inner, p_in[2], NN))
+        left2 = left2 - (p_in[2].astype(F32) - 0.5 * mm(other, p_in[3], NN))
         inverse, pieces = factored(left2)
         raw = mm(pieces, grown[...], NN)
         raw = raw - 0.5 * mm(mm(pieces, twice0, NT), right0, NN) - 0.5 * mm(mm(pieces, moved1, NT), right1, NN)
-        right2 = product_of(inverse, raw[:RANK] + raw[RANK:])
-        q_out[2] = right2.astype(BF16)
-        sent_q2 = exchange(q_out.at[2], q_in.at[2], 9, 4)
+        raw = raw[:RANK] + raw[RANK:]
+        q_out[2] = raw.astype(BF16)
+        sent_q2 = exchange(q_out.at[2], q_in.at[2], 12, 4)
+        c_out[2, :RANK, :RANK] = inverse[:RANK].astype(F32) + inverse[RANK:].astype(F32)
+        sent_i2 = exchange(c_out.at[2, pl.ds(0, RANK)], c_in.at[6, pl.ds(0, RANK)], 13, 4)
+        right2 = product_of(inverse, raw)
         basis2 = product_of(inverse, left2).astype(BF16)
         bases_ref[2 * RANK :, :] = basis2
         rights_ref[RANK : 2 * RANK, :] = right1.astype(BF16)
         started = scatter0 + scatter1 + gather0 + gather1
-        for copy in started + sent_c1 + [sent_c0, sent_p1, sent_p2, sent_m1, sent_q0, sent_q1]:
+        for copy in started + sent_c0 + sent_c1 + [sent_p1, sent_p2, sent_m0, sent_m1, sent_q0, sent_q1]:
             copy.wait_send()
+        sent_i2.wait_recv()
+        inverse = c_in[6, :RANK, :RANK]
+        top = inverse.astype(BF16)
+        inverse = jnp.concatenate([top, (inverse - top.astype(F32)).astype(BF16)], axis=0)
         sent_q2.wait_recv()
-        rights_ref[2 * RANK :, :] = (right2 - q_in[2].astype(F32)).astype(BF16)
+        other = mm(inverse, q_in[2], NN)
+        rights_ref[2 * RANK :, :] = (right2 - other[:RANK] - other[RANK:]).astype(BF16)
+        sent_i2.wait_send()
         sent_q2.wait_send()
 
     vm, dma = pltpu.VMEM, pltpu.SemaphoreType.DMA
@@ -297,12 +312,12 @@
         vm((RANK, wide), BF16), vm((2 * RANK, wide), BF16),
         vm((shards, RANK, lanes), BF16), vm((shards, 2 * RANK, lanes), BF16),
         vm((RANK, lanes), BF16), vm((2 * RANK, lanes), BF16),
-        vm((RANK, wide), BF16), vm((RANK, wide), BF16), vm((3, RANK, depth), BF16), vm((3, RANK, depth), BF16),
+        vm((RANK, wide), BF16), vm((RANK, wide), BF16), vm((4, RANK, depth), BF16), vm((4, RANK, depth), BF16),
         vm((2 * RANK, wide), BF16),
-        vm((2, 2 * RANK, 128), F32), vm((4, 2 * RANK, 128), F32),
+        vm((3, 2 * RANK, 128), F32), vm((7, 2 * RANK, 128), F32),
         vm((3, RANK, hidden), BF16), vm((3, RANK, hidden), BF16),
-        dma((2 * depth // CHUNK + 4,)), dma((2, shards)), dma((2, shards)),
-        dma((3 * shards,)), dma((3 * shards,)), dma((10,)), dma((10,)),
+        dma((depth // CHUNK + 4,)), dma((2, shards)), dma((2, shards)),
+        dma((3 * shards,)), dma((3 * shards,)), dma((14,)), dma((14,)),
     ]
     return kernel, scratch
 
@@ -337,7 +352,7 @@
             out_shape=jax.ShapeDtypeStruct((depth, hidden), BF16),
             in_specs=[in_vmem] * 3,
             out_specs=pl.BlockSpec(memory_space=pltpu.HBM),
-            scratch_shapes=[pltpu.VMEM((depth, hidden), BF16), pltpu.SemaphoreType.DMA((pl.cdiv(hidden, 256),))],
+            scratch_shapes=[pltpu.VMEM((depth, hidden), BF16), pltpu.SemaphoreType.DMA],
             compiler_params=pltpu.CompilerParams(vmem_limit_bytes=16 * 2**20),
             name="update",
         )(grown, bases, rights)[None]

time: 45.6 us -> 48.5 us (1.064)
  Pallas kernels: 45.3 us -> 48.2 us
    pallas_call x1, Pallas kernels: 42.4 us -> 44.6 us  [per_device(): pl.pallas_call(kernel, out_shape=(pltpu.VMEM((depth, hidden), BF16), jax....]
    pallas_call x1, Pallas kernels: 2.9 us -> 3.56 us  [per_device(): pl.pallas_call(update_kernel, out_shape=jax.ShapeDtypeStruct((depth, hidd...]
where the time goes in v5:
time: 48.5 us; the launch traced here: 48.4 us
  Pallas kernels  48.2 us (99%)
    pallas_call x1, Pallas kernels, per_device(): pl.pallas_call(kernel, out_shape=(pltpu.VMEM((depth, hidden), BF16), jax....  44.6 us
    pallas_call x1, Pallas kernels, per_device(): pl.pallas_call(update_kernel, out_shape=jax.ShapeDtypeStruct((depth, hidd...  3.56 us

profile of v5, /device:TPU:0, one launch (start us, length us, event | category | flops | bytes accessed | tf_op | source)
XLA Modules:
  0.0 48.4 jit_solution(16544825212611145599)
XLA Ops:
  0.0 44.6 %rounds.1 = (bf16[2560,896]{1,0:T(8,128)(2,1)S(1)}, bf16[48,2560]{1,0:T(8,128)(2,1)S(1)}, bf16[48,896]{1,0:T(8,128)(2,1)S(1)}) custom-call(bf16[2560,896]{1,0:T(8,128)(2,1)} %bitcast.5, bf16[512,2560]{1,0:T(8,128)(2,1)} %x_hbm.1, bf16[512,896]{1,0:T(8,128)(2,1)} %t_hbm.1, f32[48,896]{1,0:T(8,128)} %bitcast.6), custom_call_target="tpu_custom_call" | custom-call | tf_op jit(solution)/shard_map/rounds/pallas_call | solution.py:335
  44.6 3.6 %update.1 = bf16[2560,896]{1,0:T(8,128)(2,1)} custom-call(bf16[2560,896]{1,0:T(8,128)(2,1)S(1)} %get-tuple-element.8.grown, bf16[48,2560]{1,0:T(8,128)(2,1)S(1)} %get-tuple-element.9.bases, bf16[48,896]{1,0:T(8,128)(2,1)S(1)} %get-tuple-element.10.rights), custom_call_target="tpu_custom_call" | custom-call | tf_op jit(solution)/shard_map/update/pallas_call | solution.py:350

commit v6 on v4

--- a/solution.py
+++ b/solution.py
@@ -64,12 +64,17 @@
 
 
 def update_kernel(grown, bases, rights, out_hbm, staged, sem):
+    depth, hidden = grown.shape
+    edges = [0, *range(256, depth, 512), depth]
     copies = []
-    for number, c in enumerate(range(0, grown.shape[1], 256)):
-        columns = pl.ds(c, min(256, grown.shape[1] - c))
-        delta = mm(bases[...], rights[:, columns], TN)
-        staged[:, columns] = (grown[:, columns].astype(F32) - 0.5 * delta).astype(BF16)
-        copies.append(pltpu.make_async_copy(staged.at[:, columns], out_hbm.at[:, columns], sem.at[number]))
+    for number, (start, stop) in enumerate(zip(edges, edges[1:])):
+        rows = slice(start, stop)
+        for c in range(0, hidden, 256):
+            columns = slice(c, min(c + 256, hidden))
+            delta = mm(bases[rows, :], rights[:, columns], NN)
+            staged[rows, columns] = (grown[rows, columns].astype(F32) - delta).astype(BF16)
+        span = pl.ds(start, stop - start)
+        copies.append(pltpu.make_async_copy(staged.at[span], out_hbm.at[span], sem.at[number]))
         copies[-1].start()
     for copy in copies:
         copy.wait()
@@ -82,7 +87,7 @@
 
     def kernel(
         w_hbm, x_hbm, t_hbm, f_hbm, grown, bases_ref, rights_ref,
-        f, w, x, t, first, sums, gram_x,
+        f, w, x, xt, t, first, sums, gram_x,
         part0, part1, rs0, rs1, own0, own1, p_own, p0_in, p_out, p_in, v12, c_out, c_in, q_out, q_in,
         load_sem, rs_send, rs_recv, ag_send, ag_recv, x_send, x_recv,
     ):
@@ -101,17 +106,12 @@
             )
 
         chunks = depth // CHUNK
-        parts = [(c * CHUNK, CHUNK) for c in range(chunks - 1)]
-        parts += [(depth - CHUNK, CHUNK // 2), (depth - CHUNK // 2, CHUNK // 2)]
-        load_f, load_t = load(f_hbm, f, 0), load(t_hbm, t, 1)
-        load_f.start()
-        load_t.start()
-        loads = []
-        for number, (start, size) in enumerate(parts):
-            span = pl.ds(start, size)
-            loads.append(load(w_hbm.at[span], w.at[span], 2 + 2 * number))
-            loads.append(load(x_hbm.at[:, span], x.at[:, span], 3 + 2 * number))
-        for copy in loads:
+        load_f, load_t, load_x = load(f_hbm, f, 0), load(t_hbm, t, 1), load(x_hbm, x, 2)
+        load_w = [
+            load(w_hbm.at[pl.ds(c * CHUNK, CHUNK)], w.at[pl.ds(c * CHUNK, CHUNK)], 3 + c)
+            for c in range(chunks)
+        ]
+        for copy in [load_f] + load_w + [load_t, load_x]:
             copy.start()
 
         barrier = pltpu.get_barrier_semaphore()
@@ -124,15 +124,15 @@
         c_out[...] = jnp.zeros_like(c_out)
         load_f.wait()
         shared = f[...].astype(BF16)
+        images = []
+        for c in range(chunks):
+            load_w[c].wait()
+            images.append(mm(shared, w[c * CHUNK : (c + 1) * CHUNK, :], NT))
         load_t.wait()
         goal = mm(shared, t[...], NT)
-        images, inside = [], -goal
-        for number, (start, size) in enumerate(parts):
-            loads[2 * number].wait()
-            images.append(mm(shared, w[start : start + size, :], NT))
-            loads[2 * number + 1].wait()
-            inside = inside + mm(images[-1], x[:, start : start + size], NT)
-        image = jnp.concatenate(images, axis=1) - 0.3 * mm(inside, x[...], NN)
+        load_x.wait()
+        image = jnp.concatenate(images, axis=1)
+        image = image - 0.3 * mm(mm(image, x[...], NT) - goal, x[...], NN)
         image, goal = image.astype(BF16), goal.astype(BF16)
         part0[:, :depth] = image[:RANK]
         part0[:, depth:] = goal[:RANK]
@@ -184,18 +184,22 @@
             gather1.append(send(own1, piece(v12, s), ag_send.at[number], ag_recv.at[number], peer(0, o)))
             gather1[-1].start()
 
+        for c in range(chunks):
+            xt[c * CHUNK : (c + 1) * CHUNK, :] = x[:, c * CHUNK : (c + 1) * CHUNK].T
         for c in range(0, tokens, 256):
-            gram_x[:, c : c + 256] = mm(x[...], x[c : c + 256, :], NT).astype(BF16)
-        for step in (1, 2):
+            gram_x[:, c : c + 256] = mm(x[...], xt[:, c : c + 256], NN).astype(BF16)
+
+        def next_sum(step):
             for c, width in blocks:
                 last = sums[step - 1, :, c : c + width]
                 product = mm(gram_x[...], last, NN)
                 value = first[:, c : c + width] + last.astype(F32) - 0.3 * product
                 sums[step, :, c : c + width] = value.astype(BF16)
 
+
         def grow(c):
             rows = slice(c * CHUNK, (c + 1) * CHUNK)
-            product = mm(x[:, rows], sums[2], TN)
+            product = mm(xt[rows, :], sums[2], NN)
             grown[rows, :] = (w[rows, :].astype(F32) - 0.3 * product).astype(BF16)
 
         def exchange(source, target, number, distance):
@@ -212,12 +216,13 @@
         inner0 = mm(image, basis0, NT)
         c_out[0, :, :RANK] = inner0
         sent_c0 = exchange(c_out.at[0], c_in.at[0], 0, 1)
-        inside = mm(jnp.concatenate([image, basis0], axis=0), x[...], NT)
+        inside = mm(jnp.concatenate([image, basis0], axis=0), xt[...], NN)
         inside0 = inside[2 * RANK :]
         inside = jnp.concatenate([inside[: 2 * RANK] - v12[:, depth:].astype(F32), inside0], axis=0)
         change = 0.3 * mm(inside, x[...], NN)
         image = image.astype(F32) - change[: 2 * RANK]
         moved0 = basis0.astype(F32) - change[2 * RANK :]
+        next_sum(1)
         sent_c0.wait_recv()
         inner0 = inner0 - c_in[0, :, :RANK]
         image = image - 0.5 * mm(inner0, moved0, NN)
@@ -229,17 +234,17 @@
         q_out[0] = right0.astype(BF16)
         sent_q0 = exchange(q_out.at[0], q_in.at[0], 2, 1)
         image = image[RANK:]
-        inside = mm(jnp.concatenate([image, moved0], axis=0), x[...], NT)
+        inside = mm(jnp.concatenate([image, moved0], axis=0), xt[...], NN)
         inside = jnp.concatenate([inside[:RANK] - v12[RANK:, depth:].astype(F32), inside[RANK:]], axis=0)
         change = 0.3 * mm(inside, x[...], NN)
         next_image = image - change[:RANK]
         p_out[1] = next_image.astype(BF16)
+        twice0 = moved0 - change[RANK:]
+        next_sum(2)
+        grow(0)
+
+        sent_p1.wait_recv()
         sent_p2 = exchange(p_out.at[1], p_in.at[1], 3, 4)
-        twice0 = moved0 - change[RANK:]
-        grow(0)
-        grow(1)
-
-        sent_p1.wait_recv()
         basis1 = orthonormal(left1 - p_in[0].astype(F32))
         inner1 = mm(image, basis1, NT)
         c_out[1, :RANK, :RANK] = inner1
@@ -247,7 +252,7 @@
             exchange(c_out.at[1, pl.ds(0, RANK)], c_in.at[1 + n, pl.ds(0, RANK)], 4 + n, distance)
             for n, distance in enumerate((2, 4, 6))
         ]
-        inside1 = mm(basis1, x[...], NT)
+        inside1 = mm(basis1, xt[...], NN)
         moved1 = basis1.astype(F32) - 0.3 * mm(inside1, x[...], NN)
         p_out[2] = moved1.astype(BF16)
         sent_m1 = exchange(p_out.at[2], p_in.at[2], 7, 4)
@@ -258,11 +263,8 @@
         right1 = right1 - 0.5 * mm(mm(basis1, moved0, NT), right0, NN)
         q_out[1] = right1.astype(BF16)
         sent_q1 = exchange(q_out.at[1], q_in.at[1], 8, 2)
-        for c in range(2, chunks):
+        for c in range(1, chunks):
             grow(c)
-        bases_ref[:RANK, :] = twice0.astype(BF16)
-        bases_ref[RANK : 2 * RANK, :] = moved1.astype(BF16)
-        rights_ref[:RANK, :] = right0.astype(BF16)
 
         sent_p2.wait_recv()
         for copy in sent_c1:
@@ -277,32 +279,43 @@
         inverse, pieces = factored(left2)
         raw = mm(pieces, grown[...], NN)
         raw = raw - 0.5 * mm(mm(pieces, twice0, NT), right0, NN) - 0.5 * mm(mm(pieces, moved1, NT), right1, NN)
-        right2 = product_of(inverse, raw[:RANK] + raw[RANK:])
-        q_out[2] = right2.astype(BF16)
+        raw = raw[:RANK] + raw[RANK:]
+        q_out[2] = raw.astype(BF16)
         sent_q2 = exchange(q_out.at[2], q_in.at[2], 9, 4)
-        basis2 = product_of(inverse, left2).astype(BF16)
-        bases_ref[2 * RANK :, :] = basis2
-        rights_ref[RANK : 2 * RANK, :] = right1.astype(BF16)
+        c_out[2, :RANK, :RANK] = inverse[:RANK].astype(F32) + inverse[RANK:].astype(F32)
+        sent_i2 = exchange(c_out.at[2, pl.ds(0, RANK)], c_in.at[4, pl.ds(0, RANK)], 10, 4)
+        right2 = product_of(inverse, raw)
+        basis2 = product_of(inverse, left2)
+        bases_ref[...] = jnp.concatenate([twice0, moved1, basis2], axis=0).astype(BF16).T
+        rights_ref[:RANK, :] = (0.5 * right0).astype(BF16)
+        rights_ref[RANK : 2 * RANK, :] = (0.5 * right1).astype(BF16)
         started = scatter0 + scatter1 + gather0 + gather1
         for copy in started + sent_c1 + [sent_c0, sent_p1, sent_p2, sent_m1, sent_q0, sent_q1]:
             copy.wait_send()
+        sent_i2.wait_recv()
+        inverse = c_in[4, :RANK, :RANK]
+        top = inverse.astype(BF16)
+        inverse = jnp.concatenate([top, (inverse - top.astype(F32)).astype(BF16)], axis=0)
         sent_q2.wait_recv()
-        rights_ref[2 * RANK :, :] = (right2 - q_in[2].astype(F32)).astype(BF16)
+        other = mm(inverse, q_in[2], NN)
+        rights_ref[2 * RANK :, :] = (0.5 * (right2 - other[:RANK] - other[RANK:])).astype(BF16)
+        sent_i2.wait_send()
         sent_q2.wait_send()
 
     vm, dma = pltpu.VMEM, pltpu.SemaphoreType.DMA
     scratch = [
-        vm((3 * RANK, hidden), F32), vm((depth, hidden), BF16), vm((tokens, depth), BF16), vm((tokens, hidden), BF16),
+        vm((3 * RANK, hidden), F32), vm((depth, hidden), BF16), vm((tokens, depth), BF16), vm((depth, tokens), BF16),
+        vm((tokens, hidden), BF16),
         vm((tokens, hidden), F32), vm((3, tokens, hidden), BF16), vm((tokens, tokens), BF16),
         vm((RANK, wide), BF16), vm((2 * RANK, wide), BF16),
         vm((shards, RANK, lanes), BF16), vm((shards, 2 * RANK, lanes), BF16),
         vm((RANK, lanes), BF16), vm((2 * RANK, lanes), BF16),
         vm((RANK, wide), BF16), vm((RANK, wide), BF16), vm((3, RANK, depth), BF16), vm((3, RANK, depth), BF16),
         vm((2 * RANK, wide), BF16),
-        vm((2, 2 * RANK, 128), F32), vm((4, 2 * RANK, 128), F32),
+        vm((3, 2 * RANK, 128), F32), vm((5, 2 * RANK, 128), F32),
         vm((3, RANK, hidden), BF16), vm((3, RANK, hidden), BF16),
-        dma((2 * depth // CHUNK + 4,)), dma((2, shards)), dma((2, shards)),
-        dma((3 * shards,)), dma((3 * shards,)), dma((10,)), dma((10,)),
+        dma((depth // CHUNK + 3,)), dma((2, shards)), dma((2, shards)),
+        dma((3 * shards,)), dma((3 * shards,)), dma((11,)), dma((11,)),
     ]
     return kernel, scratch
 
@@ -321,7 +334,7 @@
             kernel,
             out_shape=(
                 pltpu.VMEM((depth, hidden), BF16),
-                jax.ShapeDtypeStruct((3 * RANK, depth), BF16),
+                jax.ShapeDtypeStruct((depth, 3 * RANK), BF16),
                 jax.ShapeDtypeStruct((3 * RANK, hidden), BF16),
             ),
             in_specs=[pl.BlockSpec(memory_space=pltpu.HBM)] * 4,
@@ -337,7 +350,7 @@
             out_shape=jax.ShapeDtypeStruct((depth, hidden), BF16),
             in_specs=[in_vmem] * 3,
             out_specs=pl.BlockSpec(memory_space=pltpu.HBM),
-            scratch_shapes=[pltpu.VMEM((depth, hidden), BF16), pltpu.SemaphoreType.DMA((pl.cdiv(hidden, 256),))],
+            scratch_shapes=[pltpu.VMEM((depth, hidden), BF16), pltpu.SemaphoreType.DMA((depth // 512 + 1,))],
             compiler_params=pltpu.CompilerParams(vmem_limit_bytes=16 * 2**20),
             name="update",
         )(grown, bases, rights)[None]

time: 45.6 us -> 44 us (0.965)
  Pallas kernels: 45.3 us -> 43.7 us
    pallas_call x1, Pallas kernels: 42.4 us -> 41.2 us  [per_device(): pl.pallas_call(kernel, out_shape=(pltpu.VMEM((depth, hidden), BF16), jax....]
where the time goes in v6:
time: 44 us; the launch traced here: 43.9 us
  Pallas kernels  43.7 us (99%)
    pallas_call x1, Pallas kernels, per_device(): pl.pallas_call(kernel, out_shape=(pltpu.VMEM((depth, hidden), BF16), jax....  41.2 us
    pallas_call x1, Pallas kernels, per_device(): pl.pallas_call(update_kernel, out_shape=jax.ShapeDtypeStruct((depth, hidd...  2.53 us

profile of v6, /device:TPU:0, one launch (start us, length us, event | category | flops | bytes accessed | tf_op | source)
XLA Modules:
  0.0 43.9 jit_solution(4702450327055126491)
XLA Ops:
  0.0 41.2 %rounds.1 = (bf16[2560,896]{1,0:T(8,128)(2,1)S(1)}, bf16[2560,48]{1,0:T(8,128)(2,1)S(1)}, bf16[48,896]{1,0:T(8,128)(2,1)S(1)}) custom-call(bf16[2560,896]{1,0:T(8,128)(2,1)} %bitcast.5, bf16[512,2560]{1,0:T(8,128)(2,1)} %x_hbm.1, bf16[512,896]{1,0:T(8,128)(2,1)} %t_hbm.1, f32[48,896]{1,0:T(8,128)} %bitcast.6), custom_call_target="tpu_custom_call" | custom-call | tf_op jit(solution)/shard_map/rounds/pallas_call | solution.py:333
  41.2 2.5 %update.1 = bf16[2560,896]{1,0:T(8,128)(2,1)} custom-call(bf16[2560,896]{1,0:T(8,128)(2,1)S(1)} %get-tuple-element.8.grown, bf16[2560,48]{1,0:T(8,128)(2,1)S(1)} %get-tuple-element.9.bases, bf16[48,896]{1,0:T(8,128)(2,1)S(1)} %get-tuple-element.10.rights), custom_call_target="tpu_custom_call" | custom-call | tf_op jit(solution)/shard_map/update/pallas_call | solution.py:348

commit v7 on v6

--- a/solution.py
+++ b/solution.py
@@ -65,7 +65,7 @@
 
 def update_kernel(grown, bases, rights, out_hbm, staged, sem):
     depth, hidden = grown.shape
-    edges = [0, *range(256, depth, 512), depth]
+    edges = list(range(0, depth + 1, 256))
     copies = []
     for number, (start, stop) in enumerate(zip(edges, edges[1:])):
         rows = slice(start, stop)
@@ -196,6 +196,7 @@
                 value = first[:, c : c + width] + last.astype(F32) - 0.3 * product
                 sums[step, :, c : c + width] = value.astype(BF16)
 
+        next_sum(1)
 
         def grow(c):
             rows = slice(c * CHUNK, (c + 1) * CHUNK)
@@ -222,7 +223,7 @@
         change = 0.3 * mm(inside, x[...], NN)
         image = image.astype(F32) - change[: 2 * RANK]
         moved0 = basis0.astype(F32) - change[2 * RANK :]
-        next_sum(1)
+        next_sum(2)
         sent_c0.wait_recv()
         inner0 = inner0 - c_in[0, :, :RANK]
         image = image - 0.5 * mm(inner0, moved0, NN)
@@ -240,8 +241,8 @@
         next_image = image - change[:RANK]
         p_out[1] = next_image.astype(BF16)
         twice0 = moved0 - change[RANK:]
-        next_sum(2)
         grow(0)
+        grow(1)
 
         sent_p1.wait_recv()
         sent_p2 = exchange(p_out.at[1], p_in.at[1], 3, 4)
@@ -257,13 +258,14 @@
         p_out[2] = moved1.astype(BF16)
         sent_m1 = exchange(p_out.at[2], p_in.at[2], 7, 4)
 
+        right1 = mm(basis1, w[...], NN) - 0.3 * mm(inside1, sums[1], NN)
+        along0 = mm(basis1, moved0, NT)
         sent_q0.wait_recv()
         right0 = right0 - q_in[0].astype(F32)
-        right1 = mm(basis1, w[...], NN) - 0.3 * mm(inside1, sums[1], NN)
-        right1 = right1 - 0.5 * mm(mm(basis1, moved0, NT), right0, NN)
+        right1 = right1 - 0.5 * mm(along0, right0, NN)
         q_out[1] = right1.astype(BF16)
         sent_q1 = exchange(q_out.at[1], q_in.at[1], 8, 2)
-        for c in range(1, chunks):
+        for c in range(2, chunks):
             grow(c)
 
         sent_p2.wait_recv()
@@ -272,13 +274,15 @@
         inner = inner1 - c_in[1, :RANK, :RANK]
         left2 = next_image - 0.5 * mm(inner, moved1, NN)
         inner = c_in[2, :RANK, :RANK] - c_in[3, :RANK, :RANK]
-        sent_q1.wait_recv()
-        right1 = right1 - q_in[1].astype(F32)
         sent_m1.wait_recv()
         left2 = left2 - (p_in[1].astype(F32) - 0.5 * mm(inner, p_in[2], NN))
         inverse, pieces = factored(left2)
         raw = mm(pieces, grown[...], NN)
-        raw = raw - 0.5 * mm(mm(pieces, twice0, NT), right0, NN) - 0.5 * mm(mm(pieces, moved1, NT), right1, NN)
+        raw = raw - 0.5 * mm(mm(pieces, twice0, NT), right0, NN)
+        along1 = mm(pieces, moved1, NT)
+        sent_q1.wait_recv()
+        right1 = right1 - q_in[1].astype(F32)
+        raw = raw - 0.5 * mm(along1, right1, NN)
         raw = raw[:RANK] + raw[RANK:]
         q_out[2] = raw.astype(BF16)
         sent_q2 = exchange(q_out.at[2], q_in.at[2], 9, 4)
@@ -350,7 +354,7 @@
             out_shape=jax.ShapeDtypeStruct((depth, hidden), BF16),
             in_specs=[in_vmem] * 3,
             out_specs=pl.BlockSpec(memory_space=pltpu.HBM),
-            scratch_shapes=[pltpu.VMEM((depth, hidden), BF16), pltpu.SemaphoreType.DMA((depth // 512 + 1,))],
+            scratch_shapes=[pltpu.VMEM((depth, hidden), BF16), pltpu.SemaphoreType.DMA((depth // 256,))],
             compiler_params=pltpu.CompilerParams(vmem_limit_bytes=16 * 2**20),
             name="update",
         )(grown, bases, rights)[None]

time: 44 us -> 43.7 us (level)
  no operation moved by 1% of the time
where the time goes in v7:
time: 43.7 us; the launch traced here: 43.6 us
  Pallas kernels  43.4 us (99%)
    pallas_call x1, Pallas kernels, per_device(): pl.pallas_call(kernel, out_shape=(pltpu.VMEM((depth, hidden), BF16), jax....  41 us
    pallas_call x1, Pallas kernels, per_device(): pl.pallas_call(update_kernel, out_shape=jax.ShapeDtypeStruct((depth, hidd...  2.48 us

profile of v7, /device:TPU:0, one launch (start us, length us, event | category | flops | bytes accessed | tf_op | source)
XLA Modules:
  0.0 43.6 jit_solution(8884543687214973751)
XLA Ops:
  0.0 41.0 %rounds.1 = (bf16[2560,896]{1,0:T(8,128)(2,1)S(1)}, bf16[2560,48]{1,0:T(8,128)(2,1)S(1)}, bf16[48,896]{1,0:T(8,128)(2,1)S(1)}) custom-call(bf16[2560,896]{1,0:T(8,128)(2,1)} %bitcast.5, bf16[512,2560]{1,0:T(8,128)(2,1)} %x_hbm.1, bf16[512,896]{1,0:T(8,128)(2,1)} %t_hbm.1, f32[48,896]{1,0:T(8,128)} %bitcast.6), custom_call_target="tpu_custom_call" | custom-call | tf_op jit(solution)/shard_map/rounds/pallas_call | solution.py:337
  41.0 2.5 %update.1 = bf16[2560,896]{1,0:T(8,128)(2,1)} custom-call(bf16[2560,896]{1,0:T(8,128)(2,1)S(1)} %get-tuple-element.8.grown, bf16[2560,48]{1,0:T(8,128)(2,1)S(1)} %get-tuple-element.9.bases, bf16[48,896]{1,0:T(8,128)(2,1)S(1)} %get-tuple-element.10.rights), custom_call_target="tpu_custom_call" | custom-call | tf_op jit(solution)/shard_map/update/pallas_call | solution.py:352
